TPU v7x, 512 devices: a whole 4x8x8 slice. The times are simulated.
512 devices in a mesh: member: 16 (over y_lo, x), space: 32 (over y_hi, z, core).
Axes of the slice: x: 4, y: 8 (y_hi: 2, y_lo: 4; y = y_hi * 4 + y_lo), z: 8, core: 2. Of those that a mesh axis runs over, the one named last changes fastest.
Arguments:
- ensemble: float32 [128, 64, 64, 128], P(None, 'space', 'member'), may hold values from -4 to 4
- source: float32 [64, 64, 128], P('space', 'member'), may hold values from -6 to 6
- obs_rows: int32 [32, 16, 1], P('space', 'member'), may hold values from 0 to 7
- obs_values: float32 [32, 16, 128], P('space', 'member'), may hold values from -3 to 3
- obs_noise: float32 [128, 32, 16, 128], P(None, 'space', 'member'), may hold values from -5 to 5
- obs_var: float32 [32, 16, 128], P('space', 'member'), may hold values from 0.05 to 2
Outputs:
- updated: float32 [128, 64, 64, 128], P(None, 'space', 'member')
- predicted: float32 [128, 32, 16, 128], P(None, 'space', 'member')
Inputs may be any that keep to these rules, and one draw needn't show every extreme that they name: `obs_rows`: entry [s, m, o] names the cell row at (s * 2 + r // 4, m * 4 + r % 4) of the first two dimensions, whose 128 cells along the third dimension are observed; rows may repeat.
All inputs are finite; a program needn't handle non-finite values.
Results may differ from a plain program's by a relative error of at most 0.0003.
Values sent between devices are 32-bit elements; how exact they have to be, the bound alone decides.
A program may use at most 64 MiB of HBM per device.

v0:
```python
import jax
import jax.numpy as jnp
from jax import lax
from jax.sharding import PartitionSpec as P

ITERS = 4


def padded_2(x, sides, width):
    for axis, dim in sides:
        devices, length = (lax.axis_size(axis), x.shape[dim])
        up = [(i, (i + 1) % devices) for i in range(devices - 1)]
        down = [(j, i) for i, j in up]
        last = lax.slice_in_dim(x, length - width, length, axis=dim)
        leading = lax.slice_in_dim(x, 0, width, axis=dim)
        before = lax.ppermute(last, axis, up)
        after = lax.ppermute(leading, axis, down)
        x = jnp.concatenate([before, x, after], axis=dim)
    return x


def from_everyone(x, axis):
    devices = lax.axis_size(axis)
    return lax.all_to_all(jnp.broadcast_to(x[None], (devices, *x.shape)), axis, 0, 0, tiled=True)


def over_copies(x, axis):
    everything = from_everyone(x, axis)
    return jnp.sum(everything, axis=0)


def joined_along(pieces, dim):
    shape = list(pieces.shape[1:])
    shape[dim] *= pieces.shape[0]
    return jnp.moveaxis(pieces, 0, dim).reshape(shape)


def collect(x, axis, dim):
    pieces = from_everyone(x, axis)
    return joined_along(pieces, dim)


def packed_total(arrays, axis):
    ends = [0]
    for a in arrays:
        ends.append(ends[-1] + a.size)
    subtotal = lax.psum(jnp.concatenate([a.ravel() for a in arrays]), axis)
    return tuple((subtotal[b:e].reshape(a.shape) for a, b, e in zip(arrays, ends, ends[1:])))


def harmonic(first_cond, second_cond):
    return 2.0 * first_cond * second_cond / (first_cond + second_cond)


def extend_cond(cond):
    widened = padded_2(cond, (("member", 2),), 1)
    return jnp.pad(widened, ((0, 0), (1, 1), (0, 0), (1, 1)))


def extend_values(values_in):
    widened = padded_2(values_in, (("member", 2),), 1)
    return jnp.pad(widened, ((0, 0), (1, 1), (0, 0), (1, 1)))


def member_dots(dot_terms):
    return over_copies(dot_terms, "member")


def face_terms(cond):
    widened = extend_cond(cond)
    edge_pad = jnp.pad(cond, ((0, 0), (1, 1), (1, 1), (1, 1)), mode="edge")
    cond_pad = jnp.where(widened > 0.0, widened, edge_pad)
    face_x = harmonic(cond_pad[:, :-1, 1:-1, 1:-1], cond_pad[:, 1:, 1:-1, 1:-1])
    face_y = harmonic(cond_pad[:, 1:-1, :-1, 1:-1], cond_pad[:, 1:-1, 1:, 1:-1])
    face_z = harmonic(cond, cond_pad[:, 1:-1, 1:-1, 2:])
    lower_z = jnp.concatenate([harmonic(cond[..., :1], cond[..., :1]), face_z[..., :-1]], axis=-1)
    return (face_x, face_y, face_z, lower_z)


def operate(values_in, face_x, face_y, face_z, lower_z):
    padded = extend_values(values_in)
    result = face_x[:, 1:] * (values_in - padded[:, 2:, 1:-1, 1:-1]) + face_x[:, :-1] * (
        values_in - padded[:, :-2, 1:-1, 1:-1]
    )
    result = (
        result
        + face_y[:, :, 1:] * (values_in - padded[:, 1:-1, 2:, 1:-1])
        + face_y[:, :, :-1] * (values_in - padded[:, 1:-1, :-2, 1:-1])
    )
    result = (
        result
        + face_z * (values_in - padded[:, 1:-1, 1:-1, 2:])
        + lower_z * (values_in - padded[:, 1:-1, 1:-1, :-2])
    )
    return result


def conjugate(cond, forcing):
    face_x, face_y, face_z, lower_z = face_terms(cond)
    residual = jnp.broadcast_to(forcing[None], cond.shape)
    direction = residual
    solution = jnp.zeros_like(cond)
    norm_now = member_dots(jnp.sum(residual * residual, axis=(1, 2, 3)))
    for iteration in range(ITERS):
        image = operate(direction, face_x, face_y, face_z, lower_z)
        step_size = norm_now / member_dots(jnp.sum(direction * image, axis=(1, 2, 3)))
        solution = solution + step_size[:, None, None, None] * direction
        residual = residual - step_size[:, None, None, None] * image
        if iteration + 1 < ITERS:
            norm_next = member_dots(jnp.sum(residual * residual, axis=(1, 2, 3)))
            direction = residual + (norm_next / norm_now)[:, None, None, None] * direction
            norm_now = norm_next
    return solution


def local(ensemble, source, obs_rows, obs_values, obs_noise, obs_var):
    total_members = ensemble.shape[0]
    block_x, block_y, layers = source.shape
    held_fields = lax.all_to_all(ensemble, "space", split_axis=0, concat_axis=1, tiled=True)
    forcing = collect(source, "space", 0)
    pressure = conjugate(jnp.exp(held_fields), forcing)
    held_count = pressure.shape[0]
    cells_flat = pressure.reshape(held_count, -1, layers)
    gathered_rows = collect(obs_rows, "space", 0)
    row_ids = gathered_rows[:, 0]
    peer_ids = jnp.arange(row_ids.shape[0], dtype=jnp.int32)[:, None]
    flat_index = (peer_ids * block_x + row_ids // block_y) * block_y + row_ids % block_y
    picked = jnp.take(cells_flat, flat_index.reshape(-1), axis=1)
    returned = lax.all_to_all(picked, "space", split_axis=1, concat_axis=0, tiled=True)
    predicted = returned.reshape(total_members, 1, 1, -1)
    flat_pred = returned.reshape(total_members, -1)
    inv_sigma = 1.0 / jnp.sqrt(obs_var.reshape(-1))
    spread = (flat_pred - jnp.mean(flat_pred, axis=0)) * inv_sigma
    misfit = (obs_values.reshape(-1) - flat_pred) * inv_sigma + obs_noise.reshape(total_members, -1)
    gram_part = jnp.dot(spread, spread.T, precision=lax.Precision.HIGHEST)
    cross_part = jnp.dot(spread, misfit.T, precision=lax.Precision.HIGHEST)
    gram_sum, cross_sum = packed_total((gram_part, cross_part), ("member", "space"))
    factor = jnp.linalg.cholesky(
        gram_sum + (total_members - 1.0) * jnp.eye(total_members, dtype=jnp.float32)
    )
    weights = jax.scipy.linalg.cho_solve((factor, True), cross_sum)
    flat_field = ensemble.reshape(total_members, -1)
    anomalies = flat_field - jnp.mean(flat_field, axis=0)
    updated = flat_field + jnp.dot(weights.T, anomalies, precision=lax.Precision.HIGHEST)
    return (updated.reshape(ensemble.shape), predicted)


def solution(mesh):
    in_specs = (
        P(None, "space", "member", None),
        P("space", "member", None),
        P("space", "member", None),
        P("space", "member", None),
        P(None, "space", "member", None),
        P("space", "member", None),
    )
    out_specs = (P(None, "space", "member", None), P(None, "space", "member", None))
    return jax.shard_map(local, mesh=mesh, in_specs=in_specs, out_specs=out_specs, check_vma=False)
```

profile of v0, /device:TPU:1, one launch (start us, length us, event | category | flops | bytes accessed | tf_op | source)
XLA Modules:
  0.0 544.3 jit_solution(13039079994435037711)
XLA Ops:
  7.2 0.7 copy.50
  7.9 29.1 %all_to_all.82 = f32[32,2,4,128]{3,1,2,0:T(2,128)S(1)} all-to-all(f32[32,2,4,128]{3,1,2,0:T(2,128)S(1)} %broadcast_in_dim.41), channel_id=1, replica_groups=mesh['member'=16,'space'=32] {'space'}, dimensions={0} | all-to-all | bytes 262144 | tf_op jit(solution)/shard_map/all_to_all | solution.py:24
  37.0 4.7 all-to-all-start.3
  41.8 3.1 collective-permute-start.2
  44.9 1.3 collective-permute-start.3
  46.2 0.7 multiply_reduce_fusion.6
  47.4 3.9 collective-permute-done.3
  51.3 1.7 select_maximum_fusion.6
  53.1 6.3 %all-to-all-done.3 = f32[128,2,4,128]{3,2,1,0:T(4,128)S(1)} async-done(((f32[128,2,4,128]{3,2,1,0:T(4,128)}), f32[128,2,4,128]{3,2,1,0:T(4,128)S(1)}, u32[]{:S(2)}, u32[]{:S(2)}) %all-to-all-start.3) | async-done | bytes 524320 | tf_op jit(solution)/shard_map/all_to_all | solution.py:119
  59.3 1.2 broadcast_in_dim.42
  60.6 9.0 %all-to-all-start.2 = ((f32[16,1,4]{2,1,0:T(1,128)}), f32[16,1,4]{2,1,0:T(1,128)S(1)}, u32[]{:S(2)}, u32[]{:S(2)}) async-start(f32[16,1,4]{2,1,0:T(1,128)} %broadcast_in_dim.42), calls=%async_computation.2 | async-start | bytes 16384 | tf_op jit(solution)/shard_map/all_to_all | solution.py:24
  70.1 0.7 fusion.87
  71.2 3.3 collective-permute-start
  74.5 1.3 collective-permute-start.1
  76.0 1.1 copy.55
  77.1 3.3 collective-permute-done.1
  80.4 1.8 compare_select_fusion
  83.3 0.8 copy-done
  84.2 0.9 multiply_reduce_fusion.5
  85.2 0.6 broadcast_in_dim.47
  85.8 7.7 %all-to-all-start.4 = ((f32[16,1,4]{2,1,0:T(1,128)}), f32[16,1,4]{2,1,0:T(1,128)S(1)}, u32[]{:S(2)}, u32[]{:S(2)}) async-start(f32[16,1,4]{2,1,0:T(1,128)} %broadcast_in_dim.47), calls=%async_computation.4 | async-start | bytes 16384 | tf_op jit(solution)/shard_map/all_to_all | solution.py:24
  93.5 6.7 %all-to-all-done.4 = f32[16,1,4]{2,1,0:T(1,128)S(1)} async-done(((f32[16,1,4]{2,1,0:T(1,128)}), f32[16,1,4]{2,1,0:T(1,128)S(1)}, u32[]{:S(2)}, u32[]{:S(2)}) %all-to-all-start.4) | async-done | bytes 288 | tf_op jit(solution)/shard_map/all_to_all | solution.py:24
  100.5 9.4 %all_to_all.83 = f32[16,1,4]{2,1,0:T(1,128)S(1)} all-to-all(f32[16,1,4]{2,1,0:T(1,128)S(1)} %broadcast_in_dim.48), channel_id=1, replica_groups=mesh['member'=16,'space'=32] {'member'}, dimensions={0} | all-to-all | bytes 512 | tf_op jit(solution)/shard_map/all_to_all | solution.py:24
  110.1 2.2 collective-permute-start.4
  112.3 1.3 collective-permute-start.5
  114.2 3.8 collective-permute-done.5
  118.6 1.4 multiply_reduce_fusion.3
  120.0 12.4 %all_to_all.84 = f32[16,1,4]{2,1,0:T(1,128)S(1)} all-to-all(f32[16,1,4]{2,1,0:T(1,128)S(1)} %broadcast_in_dim.49), channel_id=1, replica_groups=mesh['member'=16,'space'=32] {'member'}, dimensions={0} | all-to-all | bytes 512 | tf_op jit(solution)/shard_map/all_to_all | solution.py:24
  132.4 1.3 multiply_reduce_fusion.2
  133.8 9.4 %all_to_all.85 = f32[16,1,4]{2,1,0:T(1,128)S(1)} all-to-all(f32[16,1,4]{2,1,0:T(1,128)S(1)} %broadcast_in_dim.50), channel_id=1, replica_groups=mesh['member'=16,'space'=32] {'member'}, dimensions={0} | all-to-all | bytes 512 | tf_op jit(solution)/shard_map/all_to_all | solution.py:24
  143.4 0.7 fusion.84
  144.1 2.8 collective-permute-start.6
  146.9 1.3 collective-permute-start.7
  149.4 17.0 %all-to-all-start = ((s32[32,1,1,1]{3,2,1,0:T(1,128)}), s32[32,1,1,1]{3,2,1,0:T(1,128)S(1)}, u32[]{:S(2)}, u32[]{:S(2)}) async-start(s32[32,1,1,1]{3,2,1,0:T(1,128)} %broadcast_in_dim.39), calls=%async_computation | async-start | bytes 32768 | tf_op jit(solution)/shard_map/all_to_all | solution.py:24
  166.5 1.5 select_maximum_fusion.2
  168.1 2.4 multiply_reduce_fusion.1
  170.4 7.7 %all-to-all-done = s32[32,1,1,1]{3,2,1,0:T(1,128)S(1)} async-done(((s32[32,1,1,1]{3,2,1,0:T(1,128)}), s32[32,1,1,1]{3,2,1,0:T(1,128)S(1)}, u32[]{:S(2)}, u32[]{:S(2)}) %all-to-all-start) | async-done | bytes 160 | tf_op jit(solution)/shard_map/all_to_all | solution.py:24
  178.7 5.2 all-to-all-start.8
  184.0 1.2 reduce_sum.179
  185.2 0.7 reduce.20
  185.8 4.9 all-to-all-done.8
  190.7 1.3 multiply_reduce_fusion
  192.6 3.5 all-to-all-start.9
  196.1 6.7 %all-to-all-done.9 = f32[16,1,4]{2,1,0:T(1,128)S(1)} async-done(((f32[16,1,4]{2,1,0:T(1,128)}), f32[16,1,4]{2,1,0:T(1,128)S(1)}, u32[]{:S(2)}, u32[]{:S(2)}) %all-to-all-start.9) | async-done | bytes 288 | tf_op jit(solution)/shard_map/all_to_all | solution.py:24
  202.8 1.4 multiply_add_fusion.1
  204.3 2.3 collective-permute-start.8
  206.6 1.3 collective-permute-start.9
  208.5 3.8 collective-permute-done.9
  212.9 0.7 fusion.14
  214.2 5.8 %all-to-all-start.10 = ((f32[16,1,4]{2,1,0:T(1,128)}), f32[16,1,4]{2,1,0:T(1,128)S(1)}, u32[]{:S(2)}, u32[]{:S(2)}) async-start(f32[16,1,4]{2,1,0:T(1,128)} %broadcast_in_dim.53), calls=%async_computation.10 | async-start | bytes 16384 | tf_op jit(solution)/shard_map/all_to_all | solution.py:24
  220.0 6.7 %all-to-all-done.10 = f32[16,1,4]{2,1,0:T(1,128)S(1)} async-done(((f32[16,1,4]{2,1,0:T(1,128)}), f32[16,1,4]{2,1,0:T(1,128)S(1)}, u32[]{:S(2)}, u32[]{:S(2)}) %all-to-all-start.10) | async-done | bytes 288 | tf_op jit(solution)/shard_map/all_to_all | solution.py:24
  228.0 0.7 select_bitcast_fusion
  228.8 9.9 %all-to-all-start.11 = ((f32[4,32,128]{2,0,1:T(4,128)}), f32[4,32,128]{2,0,1:T(4,128)S(1)}, u32[]{:S(2)}, u32[]{:S(2)}) async-start(f32[4,32,128]{2,0,1:T(4,128)} %select_bitcast_fusion), calls=%async_computation.11 | async-start | bytes 131072 | tf_op jit(solution)/shard_map/all_to_all | solution.py:129
  238.8 11.8 %all-to-all-done.11 = f32[4,32,128]{2,0,1:T(4,128)S(1)} async-done(((f32[4,32,128]{2,0,1:T(4,128)}), f32[4,32,128]{2,0,1:T(4,128)S(1)}, u32[]{:S(2)}, u32[]{:S(2)}) %all-to-all-start.11) | async-done | bytes 65568 | tf_op jit(solution)/shard_map/all_to_all | solution.py:129
  251.2 0.7 pad_maximum_fusion.14
  252.2 256.9 %all-reduce.7.cloned.1.call-done = f32[32768]{0:T(1024)} async-done(((f32[32768]{0:T(1024)}), f32[32768]{0:T(1024)}) %all-reduce.7.cloned.1.call-update) | async-done | bytes 131088 | tf_op jit(solution)/shard_map/psum | solution.py:47
  509.1 0.9 fusion.69
  510.1 0.9 fusion.73
  510.9 11.7 %cholesky.16 = f32[128,128]{1,0:T(8,128)S(1)} custom-call(f32[128,128]{1,0:T(8,128)S(1)} %fusion.73), custom_call_target="Cholesky" | custom-call | tf_op jit(solution)/shard_map/jit(cholesky)/cholesky | solution.py:138
  522.7 0.6 compare_reduce_fusion
  523.3 0.7 fusion.67
  524.0 9.8 %custom-call.10 = f32[1,128,128]{1,2,0:T(8,128)S(1)} custom-call(f32[1,128,128]{2,1,0:T(8,128)S(1)} %fusion.67), custom_call_target="InvertDiagBlocksLowerTriangular" | custom-call | tf_op jit(solution)/shard_map/jit(_cho_solve)/triangular_solve | solution.py:141
  533.8 1.1 fusion.68
  535.8 1.0 reshape.469
  (102 shorter events, 12.4 us)
Async XLA Ops:
  37.0 22.4 %all-to-all-start.3 = ((f32[128,2,4,128]{3,2,1,0:T(4,128)}), f32[128,2,4,128]{3,2,1,0:T(4,128)S(1)}, u32[]{:S(2)}, u32[]{:S(2)}) async-start(f32[128,2,4,128]{3,2,1,0:T(4,128)} %param.6), calls=%async_computation.3 | async-start | bytes 1048576 | tf_op jit(solution)/shard_map/all_to_all | solution.py:119
  41.8 5.6 %collective-permute-start.2 = (f32[4,64,1,128]{3,1,2,0:T(8,128)S(1)}, f32[4,64,1,128]{3,1,2,0:T(8,128)S(1)}, u32[]{:S(2)}, u32[]{:S(2)}) collective-permute-start(f32[4,64,1,128]{3,1,2,0:T(8,128)S(1)} %broadcast_in_dim.45), channel_id=1, source_target_pairs={{0,32},{32,64},{64,96},{96,128},{128,160},{160,192},{192,224},{224... | collective-permute-start | bytes 393224 | tf_op jit(solution)/shard_map/ppermute | solution.py:16
  44.9 6.3 %collective-permute-start.3 = (f32[4,64,1,128]{3,1,2,0:T(8,128)S(1)}, f32[4,64,1,128]{3,1,2,0:T(8,128)S(1)}, u32[]{:S(2)}, u32[]{:S(2)}) collective-permute-start(f32[4,64,1,128]{3,1,2,0:T(8,128)S(1)} %broadcast_in_dim.46), channel_id=1, source_target_pairs={{32,0},{64,32},{96,64},{128,96},{160,128},{192,160},{224,192},{256... | collective-permute-start | bytes 393224 | tf_op jit(solution)/shard_map/ppermute | solution.py:17
  47.4 13.2 %copy-start.7 = (f32[4,64,1,128]{3,1,2,0:T(8,128)}, f32[4,64,1,128]{3,1,2,0:T(8,128)S(1)}, u32[]{:S(2)}) copy-start(f32[4,64,1,128]{3,1,2,0:T(8,128)S(1)} %collective-permute-done.2) | copy-start | bytes 393220
  51.3 9.3 %copy-start.9 = (f32[4,64,1,128]{3,1,2,0:T(8,128)}, f32[4,64,1,128]{3,1,2,0:T(8,128)S(1)}, u32[]{:S(2)}) copy-start(f32[4,64,1,128]{3,1,2,0:T(8,128)S(1)} %collective-permute-done.3) | copy-start | bytes 393220
  60.6 24.6 %all-to-all-start.2 = ((f32[16,1,4]{2,1,0:T(1,128)}), f32[16,1,4]{2,1,0:T(1,128)S(1)}, u32[]{:S(2)}, u32[]{:S(2)}) async-start(f32[16,1,4]{2,1,0:T(1,128)} %broadcast_in_dim.42), calls=%async_computation.2 | async-start | bytes 16384 | tf_op jit(solution)/shard_map/all_to_all | solution.py:24
  71.2 5.9 %collective-permute-start = (f32[4,64,1,128]{3,1,2,0:T(8,128)}, f32[4,64,1,128]{3,1,2,0:T(8,128)S(1)}, u32[]{:S(2)}, u32[]{:S(2)}) collective-permute-start(f32[4,64,1,128]{3,1,2,0:T(8,128)} %get-tuple-element.35), channel_id=1, source_target_pairs={{0,32},{32,64},{64,96},{96,128},{128,160},{160,192},{192,224},{224... | collective-permute-start | bytes 393224 | tf_op jit(solution)/shard_map/ppermute | solution.py:16
  74.5 5.9 %collective-permute-start.1 = (f32[4,64,1,128]{3,1,2,0:T(8,128)}, f32[4,64,1,128]{3,1,2,0:T(8,128)S(1)}, u32[]{:S(2)}, u32[]{:S(2)}) collective-permute-start(f32[4,64,1,128]{3,1,2,0:T(8,128)} %get-tuple-element.36), channel_id=1, source_target_pairs={{32,0},{64,32},{96,64},{128,96},{160,128},{192,160},{224,192},{256... | collective-permute-start | bytes 393224 | tf_op jit(solution)/shard_map/ppermute | solution.py:17
  82.6 1.5 copy-start
  82.6 1.6 copy-start.6
  82.6 1.6 copy-start.8
  82.6 1.6 copy-start.10
  85.2 33.4 %copy-start.2 = (f32[4,64,4,128]{3,1,2,0:T(8,128)}, f32[4,64,4,128]{3,1,2,0:T(8,128)S(1)}, u32[]{:S(2)}) copy-start(f32[4,64,4,128]{3,1,2,0:T(8,128)S(1)} %get-tuple-element.22) | copy-start | bytes 1572868
  85.8 14.4 %all-to-all-start.4 = ((f32[16,1,4]{2,1,0:T(1,128)}), f32[16,1,4]{2,1,0:T(1,128)S(1)}, u32[]{:S(2)}, u32[]{:S(2)}) async-start(f32[16,1,4]{2,1,0:T(1,128)} %broadcast_in_dim.47), calls=%async_computation.4 | async-start | bytes 16384 | tf_op jit(solution)/shard_map/all_to_all | solution.py:24
  110.1 4.1 collective-permute-start.4
  112.3 5.7 %collective-permute-start.5 = (f32[4,64,1,128]{3,1,2,0:T(8,128)S(1)}, f32[4,64,1,128]{3,1,2,0:T(8,128)S(1)}, u32[]{:S(2)}, u32[]{:S(2)}) collective-permute-start(f32[4,64,1,128]{3,1,2,0:T(8,128)S(1)} %get-tuple-element.32), channel_id=1, source_target_pairs={{32,0},{64,32},{96,64},{128,96},{160,128},{192,160},{224,192},{256... | collective-permute-start | bytes 393224 | tf_op jit(solution)/shard_map/ppermute | solution.py:17
  133.7 57.0 %copy-start.1 = (f32[4,64,4,128]{3,1,2,0:T(8,128)}, f32[4,64,4,128]{3,1,2,0:T(8,128)S(1)}, u32[]{:S(2)}) copy-start(f32[4,64,4,128]{3,1,2,0:T(8,128)S(1)} %get-tuple-element.17) | copy-start | bytes 1572868
  144.1 22.4 %collective-permute-start.6 = (f32[4,64,1,128]{3,1,2,0:T(8,128)}, f32[4,64,1,128]{3,1,2,0:T(8,128)}, u32[]{:S(2)}, u32[]{:S(2)}) collective-permute-start(f32[4,64,1,128]{3,1,2,0:T(8,128)} %get-tuple-element.29), channel_id=1, source_target_pairs={{0,32},{32,64},{64,96},{96,128},{128,160},{160,192},{192,224},{224... | collective-permute-start | bytes 393224 | tf_op jit(solution)/shard_map/ppermute | solution.py:16
  146.9 19.6 %collective-permute-start.7 = (f32[4,64,1,128]{3,1,2,0:T(8,128)}, f32[4,64,1,128]{3,1,2,0:T(8,128)}, u32[]{:S(2)}, u32[]{:S(2)}) collective-permute-start(f32[4,64,1,128]{3,1,2,0:T(8,128)} %get-tuple-element.30), channel_id=1, source_target_pairs={{32,0},{64,32},{96,64},{128,96},{160,128},{192,160},{224,192},{256... | collective-permute-start | bytes 393224 | tf_op jit(solution)/shard_map/ppermute | solution.py:17
  149.4 28.7 %all-to-all-start = ((s32[32,1,1,1]{3,2,1,0:T(1,128)}), s32[32,1,1,1]{3,2,1,0:T(1,128)S(1)}, u32[]{:S(2)}, u32[]{:S(2)}) async-start(s32[32,1,1,1]{3,2,1,0:T(1,128)} %broadcast_in_dim.39), calls=%async_computation | async-start | bytes 32768 | tf_op jit(solution)/shard_map/all_to_all | solution.py:24
  166.5 1.6 copy-start.3
  178.7 11.9 %all-to-all-start.8 = ((f32[16,1,4]{2,1,0:T(1,128)}), f32[16,1,4]{2,1,0:T(1,128)S(1)}, u32[]{:S(2)}, u32[]{:S(2)}) async-start(f32[16,1,4]{2,1,0:T(1,128)} %broadcast_in_dim.51), calls=%async_computation.8 | async-start | bytes 16384 | tf_op jit(solution)/shard_map/all_to_all | solution.py:24
  192.6 10.2 %all-to-all-start.9 = ((f32[16,1,4]{2,1,0:T(1,128)}), f32[16,1,4]{2,1,0:T(1,128)S(1)}, u32[]{:S(2)}, u32[]{:S(2)}) async-start(f32[16,1,4]{2,1,0:T(1,128)} %broadcast_in_dim.52), calls=%async_computation.9 | async-start | bytes 16384 | tf_op jit(solution)/shard_map/all_to_all | solution.py:24
  204.2 8.6 %copy-start.4 = (f32[4,64,4,128]{3,1,2,0:T(8,128)S(1)}, f32[4,64,4,128]{3,1,2,0:T(8,128)}, u32[]{:S(2)}) copy-start(f32[4,64,4,128]{3,1,2,0:T(8,128)} %copy-done.2) | copy-start | bytes 1572868
  204.3 4.3 collective-permute-start.8
  206.6 5.7 %collective-permute-start.9 = (f32[4,64,1,128]{3,1,2,0:T(8,128)S(1)}, f32[4,64,1,128]{3,1,2,0:T(8,128)S(1)}, u32[]{:S(2)}, u32[]{:S(2)}) collective-permute-start(f32[4,64,1,128]{3,1,2,0:T(8,128)S(1)} %get-tuple-element.28), channel_id=1, source_target_pairs={{32,0},{64,32},{96,64},{128,96},{160,128},{192,160},{224,192},{256... | collective-permute-start | bytes 393224 | tf_op jit(solution)/shard_map/ppermute | solution.py:17
  214.2 12.6 %all-to-all-start.10 = ((f32[16,1,4]{2,1,0:T(1,128)}), f32[16,1,4]{2,1,0:T(1,128)S(1)}, u32[]{:S(2)}, u32[]{:S(2)}) async-start(f32[16,1,4]{2,1,0:T(1,128)} %broadcast_in_dim.53), calls=%async_computation.10 | async-start | bytes 16384 | tf_op jit(solution)/shard_map/all_to_all | solution.py:24
  226.8 12.0 %copy-start.13 = (f32[1,1,128]{2,1,0:T(1,128)S(1)}, f32[1,1,128]{2,1,0:T(1,128)}, u32[]{:S(2)}) copy-start(f32[1,1,128]{2,1,0:T(1,128)} %param.11) | copy-start | bytes 1540
  226.8 24.1 %copy-start.11 = (f32[128,1,1,128]{3,2,1,0:T(1,128)S(1)}, f32[128,1,1,128]{3,2,1,0:T(1,128)}, u32[]{:S(2)}) copy-start(f32[128,1,1,128]{3,2,1,0:T(1,128)} %param.10) | copy-start | bytes 196612
  226.8 24.1 %copy-start.12 = (f32[1,1,128]{2,1,0:T(1,128)S(1)}, f32[1,1,128]{2,1,0:T(1,128)}, u32[]{:S(2)}) copy-start(f32[1,1,128]{2,1,0:T(1,128)} %param.9) | copy-start | bytes 1540
  227.1 24.9 %copy-start.5 = (f32[128,2,4,128]{3,2,1,0:T(4,128)S(1)}, f32[128,2,4,128]{3,2,1,0:T(4,128)}, u32[]{:S(2)}) copy-start(f32[128,2,4,128]{3,2,1,0:T(4,128)} %param.6) | copy-start | bytes 1572868
  228.8 21.8 %all-to-all-start.11 = ((f32[4,32,128]{2,0,1:T(4,128)}), f32[4,32,128]{2,0,1:T(4,128)S(1)}, u32[]{:S(2)}, u32[]{:S(2)}) async-start(f32[4,32,128]{2,0,1:T(4,128)} %select_bitcast_fusion), calls=%async_computation.11 | async-start | bytes 131072 | tf_op jit(solution)/shard_map/all_to_all | solution.py:129
  238.7 270.4 %all-reduce.7.cloned.1.call-start = ((), (), s32[]{:S(2)}) async-start(), calls=%async_computation.12 | async-start | bytes 262144 | tf_op jit(solution)/shard_map/psum | solution.py:47
Sparse Core Ops, SparseCore 0:
  252.1 257.0 all-reduce.6
where the time goes:
time: 546 us; the launch traced here: 544 us
  waiting for transfers between devices  324 us (59%)
  starting transfers between devices  83.1 us (15%)
  blocking collectives  60.2 us (11%)
  other arithmetic  46.6 us (9%)
  between operations  15.3 us (3%)
  local copies, waits for them, and re-layouts  12.6 us (2%)
    psum x1, waiting for transfers between devices, packed_total(): subtotal = lax.psum(jnp.concatenate([a.ravel() for a in arrays]), axis)  257 us
    all_to_all x4, blocking collectives, from_everyone(): lax.all_to_all(jnp.broadcast_to(x[None], (devices, *x.shape)), axis, 0, 0...  60.2 us
    all_to_all x6, starting transfers between devices, from_everyone(): lax.all_to_all(jnp.broadcast_to(x[None], (devices, *x.shape)), axis, 0, 0...  48.2 us
    all_to_all x6, waiting for transfers between devices, from_everyone(): lax.all_to_all(jnp.broadcast_to(x[None], (devices, *x.shape)), axis, 0, 0...  32.6 us
    ppermute x5, waiting for transfers between devices, padded_2(): after = lax.ppermute(leading, axis, down)  14.8 us
    ppermute x5, starting transfers between devices, padded_2(): before = lax.ppermute(last, axis, up)  13.8 us
    another operation x3, other arithmetic, local(): jnp.linalg.cholesky(gram_sum + (total_members - 1.0) * jnp.eye(total_memb...  12.4 us
    all_to_all x1, waiting for transfers between devices, local(): lax.all_to_all(picked, 'space', split_axis=1, concat_axis=0, tiled=True)  11.8 us
  transfers between devices with their start and end apart: 19, of which 15 were waited for; matrix products, arithmetic and copies ran while one was open for 3% of the time, Pallas kernels for 0%

commit v1 on v0

--- a/solution.py
+++ b/solution.py
@@ -1,7 +1,12 @@
 import jax
 import jax.numpy as jnp
 from jax import lax
+from jax.experimental import pallas as pl
+from jax.experimental.pallas import tpu as pltpu
 from jax.sharding import PartitionSpec as P
+
+X, Y_LO, Y_HI, Z, CORES = 4, 4, 2, 8, 2
+WIDE = 8
 
 ITERS = 4
 
@@ -40,12 +45,115 @@
     return joined_along(pieces, dim)
 
 
-def packed_total(arrays, axis):
-    ends = [0]
-    for a in arrays:
-        ends.append(ends[-1] + a.size)
-    subtotal = lax.psum(jnp.concatenate([a.ravel() for a in arrays]), axis)
-    return tuple((subtotal[b:e].reshape(a.shape) for a, b, e in zip(arrays, ends, ends[1:])))
+def place():
+    member = lax.axis_index("member")
+    space = lax.axis_index("space")
+    x = lax.rem(member, X)
+    y = lax.div(space, Z * CORES) * Y_LO + lax.div(member, X)
+    z = lax.rem(lax.div(space, CORES), Z)
+    return x, y, z, lax.rem(space, CORES)
+
+
+def device_at(x, y, z, core):
+    member = lax.rem(y, Y_LO) * X + x
+    space = (lax.div(y, Y_LO) * Z + z) * CORES + core
+    return {"member": member, "space": space}
+
+
+def sum_kernel(part, total, got_row, sum_row, got_y, sum_y, got_z, all_y, all_row, send_sems, recv_sems):
+    x, y, z, core = place()
+    row = x * CORES + core
+
+    def row_peer(step):
+        other = lax.rem(row + step, WIDE)
+        return other, device_at(lax.div(other, CORES), y, z, lax.rem(other, CORES))
+
+    def y_peer(step):
+        other = lax.rem(y + step, WIDE)
+        return other, device_at(x, other, z, core)
+
+    def z_peer(step):
+        other = lax.rem(z + step, WIDE)
+        return other, device_at(x, y, other, core)
+
+    barrier = pltpu.get_barrier_semaphore()
+    for peer in (row_peer, y_peer, z_peer):
+        for step in range(1, WIDE):
+            pl.semaphore_signal(barrier, inc=1, device_id=peer(step)[1], device_id_type=pl.DeviceIdType.MESH)
+    pl.semaphore_wait(barrier, 3 * (WIDE - 1))
+
+    def exchange(phase, peer, source, target):
+        copies = []
+        for step in range(1, WIDE):
+            other, device = peer(step)
+            copy = pltpu.make_async_remote_copy(
+                src_ref=source(other),
+                dst_ref=target(step),
+                send_sem=send_sems.at[phase, step - 1],
+                recv_sem=recv_sems.at[phase, step - 1],
+                device_id=device,
+                device_id_type=pl.DeviceIdType.MESH,
+            )
+            copy.start()
+            copies.append(copy)
+        return copies
+
+    def arrived(copies):
+        for copy in copies:
+            copy.wait_recv()
+
+    sent = []
+    copies = exchange(0, row_peer, lambda o: part.at[pl.ds(o * WIDE, WIDE)], lambda s: got_row.at[s - 1])
+    sent += copies
+    arrived(copies)
+    sum_row[...] = part[pl.ds(row * WIDE, WIDE)] + jnp.sum(got_row[...], axis=0)
+
+    copies = exchange(1, y_peer, lambda o: sum_row.at[o], lambda s: got_y.at[s - 1])
+    sent += copies
+    arrived(copies)
+    sum_y[...] = sum_row[y] + jnp.sum(got_y[...], axis=0)
+
+    got_z[z] = sum_y[...]
+    copies = exchange(2, z_peer, lambda o: sum_y, lambda s: got_z.at[z])
+    sent += copies
+    arrived(copies)
+    sum_y_z = jnp.sum(got_z[...], axis=0)
+    all_y[y] = sum_y_z
+
+    copies = exchange(3, y_peer, lambda o: all_y.at[y], lambda s: all_y.at[y])
+    sent += copies
+    arrived(copies)
+
+    copies = exchange(4, row_peer, lambda o: all_y, lambda s: all_row.at[row])
+    sent += copies
+    all_row[row] = all_y[...]
+    arrived(copies)
+    total[...] = all_row[...].reshape(total.shape)
+    for copy in sent:
+        copy.wait_send()
+
+
+def sum_everywhere(part):
+    dims = part.shape[1:]
+    return pl.pallas_call(
+        sum_kernel,
+        out_shape=jax.ShapeDtypeStruct(part.shape, jnp.float32),
+        in_specs=[pl.BlockSpec(memory_space=pltpu.VMEM)],
+        out_specs=pl.BlockSpec(memory_space=pltpu.VMEM),
+        scratch_shapes=[
+            pltpu.VMEM((WIDE - 1, WIDE, *dims), jnp.float32),
+            pltpu.VMEM((WIDE, *dims), jnp.float32),
+            pltpu.VMEM((WIDE - 1, *dims), jnp.float32),
+            pltpu.VMEM(dims, jnp.float32),
+            pltpu.VMEM((WIDE, *dims), jnp.float32),
+            pltpu.VMEM((WIDE, *dims), jnp.float32),
+            pltpu.VMEM((WIDE, WIDE, *dims), jnp.float32),
+            pltpu.SemaphoreType.DMA((5, WIDE - 1)),
+            pltpu.SemaphoreType.DMA((5, WIDE - 1)),
+        ],
+        compiler_params=pltpu.CompilerParams(collective_id=1, has_side_effects=True),
+        name="sum_everywhere",
+    )(part)
 
 
 def harmonic(first_cond, second_cond):
@@ -134,7 +242,8 @@
     misfit = (obs_values.reshape(-1) - flat_pred) * inv_sigma + obs_noise.reshape(total_members, -1)
     gram_part = jnp.dot(spread, spread.T, precision=lax.Precision.HIGHEST)
     cross_part = jnp.dot(spread, misfit.T, precision=lax.Precision.HIGHEST)
-    gram_sum, cross_sum = packed_total((gram_part, cross_part), ("member", "space"))
+    both = sum_everywhere(jnp.concatenate([gram_part, cross_part]).reshape(64, 4, -1))
+    gram_sum, cross_sum = jnp.split(both.reshape(2 * total_members, total_members), 2)
     factor = jnp.linalg.cholesky(
         gram_sum + (total_members - 1.0) * jnp.eye(total_members, dtype=jnp.float32)
     )

time: 546 us -> 303 us (0.55)
  waiting for transfers between devices: 324 us -> 65.1 us
  Pallas kernels: 0 us -> 27.9 us
  between operations: 15.3 us -> 1.89 us
    psum x1 -> x0, waiting for transfers between devices: 257 us -> none  [packed_total(): subtotal = lax.psum(jnp.concatenate([a.ravel() for a in arrays]), axis)]
    pallas_call x0 -> x1, Pallas kernels: none -> 27.9 us  [sum_everywhere(): pl.pallas_call(sum_kernel, out_shape=jax.ShapeDtypeStruct(part.shape, jnp...]
  transfers between devices with their start and end apart: 19 -> 18, of which waited for: 15 -> 14; matrix products, arithmetic and copies ran while one was open for 3% -> 6% of each run, Pallas kernels for 0% -> 0%
where the time goes in v1:
time: 303 us; the launch traced here: 301 us
  starting transfers between devices  84.3 us (28%)
  waiting for transfers between devices  65.1 us (21%)
  blocking collectives  60.2 us (20%)
  other arithmetic  44.9 us (15%)
  Pallas kernels  27.9 us (9%)
  local copies, waits for them, and re-layouts  15.3 us (5%)
    all_to_all x4, blocking collectives, from_everyone(): lax.all_to_all(jnp.broadcast_to(x[None], (devices, *x.shape)), axis, 0, 0...  60.2 us
    all_to_all x6, starting transfers between devices, from_everyone(): lax.all_to_all(jnp.broadcast_to(x[None], (devices, *x.shape)), axis, 0, 0...  48.2 us
    all_to_all x6, waiting for transfers between devices, from_everyone(): lax.all_to_all(jnp.broadcast_to(x[None], (devices, *x.shape)), axis, 0, 0...  30.5 us
    pallas_call x1, Pallas kernels, sum_everywhere(): pl.pallas_call(sum_kernel, out_shape=jax.ShapeDtypeStruct(part.shape, jnp...  27.9 us
    ppermute x5, waiting for transfers between devices, padded_2(): after = lax.ppermute(leading, axis, down)  14.8 us
    ppermute x5, starting transfers between devices, padded_2(): before = lax.ppermute(last, axis, up)  13.8 us
    another operation x3, other arithmetic, local(): jnp.linalg.cholesky(gram_sum + (total_members - 1.0) * jnp.eye(total_memb...  12.4 us
    all_to_all x1, waiting for transfers between devices, local(): lax.all_to_all(picked, 'space', split_axis=1, concat_axis=0, tiled=True)  11.8 us
  transfers between devices with their start and end apart: 18, of which 14 were waited for; matrix products, arithmetic and copies ran while one was open for 6% of the time, Pallas kernels for 0%

profile of v1, /device:TPU:1, one launch (start us, length us, event | category | flops | bytes accessed | tf_op | source)
XLA Modules:
  0.0 301.3 jit_solution(8700185604118259570)
XLA Ops:
  0.6 0.7 copy.50
  1.4 29.1 %all_to_all.82 = f32[32,2,4,128]{3,1,2,0:T(2,128)S(1)} all-to-all(f32[32,2,4,128]{3,1,2,0:T(2,128)S(1)} %broadcast_in_dim.41), channel_id=1, replica_groups=mesh['member'=16,'space'=32] {'space'}, dimensions={0} | all-to-all | bytes 262144 | tf_op jit(solution)/shard_map/all_to_all | solution.py:29
  30.5 4.7 %all-to-all-start.3 = ((f32[128,2,4,128]{3,2,1,0:T(4,128)}), f32[128,2,4,128]{3,2,1,0:T(4,128)S(1)}, u32[]{:S(2)}, u32[]{:S(2)}) async-start(f32[128,2,4,128]{3,2,1,0:T(4,128)} %param.6), calls=%async_computation.3 | async-start | bytes 1048576 | tf_op jit(solution)/shard_map/all_to_all | solution.py:227
  35.2 3.1 %collective-permute-start.2 = (f32[4,64,1,128]{3,1,2,0:T(8,128)S(1)}, f32[4,64,1,128]{3,1,2,0:T(8,128)S(1)}, u32[]{:S(2)}, u32[]{:S(2)}) collective-permute-start(f32[4,64,1,128]{3,1,2,0:T(8,128)S(1)} %broadcast_in_dim.45), channel_id=1, source_target_pairs={{0,32},{32,64},{64,96},{96,128},{128,160},{160,192},{192,224},{224... | collective-permute-start | bytes 393224 | tf_op jit(solution)/shard_map/ppermute | solution.py:21
  38.4 1.3 collective-permute-start.3
  39.7 0.7 multiply_reduce_fusion.6
  40.9 3.9 %collective-permute-done.3 = f32[4,64,1,128]{3,1,2,0:T(8,128)S(1)} collective-permute-done((f32[4,64,1,128]{3,1,2,0:T(8,128)S(1)}, f32[4,64,1,128]{3,1,2,0:T(8,128)S(1)}, u32[]{:S(2)}, u32[]{:S(2)}) %collective-permute-start.3) | collective-permute-done | bytes 131104 | tf_op jit(solution)/shard_map/ppermute | solution.py:22
  44.8 1.7 select_maximum_fusion.6
  46.5 6.3 %all-to-all-done.3 = f32[128,2,4,128]{3,2,1,0:T(4,128)S(1)} async-done(((f32[128,2,4,128]{3,2,1,0:T(4,128)}), f32[128,2,4,128]{3,2,1,0:T(4,128)S(1)}, u32[]{:S(2)}, u32[]{:S(2)}) %all-to-all-start.3) | async-done | bytes 524320 | tf_op jit(solution)/shard_map/all_to_all | solution.py:227
  52.8 1.2 broadcast_in_dim.42
  54.1 9.0 %all-to-all-start.2 = ((f32[16,1,4]{2,1,0:T(1,128)}), f32[16,1,4]{2,1,0:T(1,128)S(1)}, u32[]{:S(2)}, u32[]{:S(2)}) async-start(f32[16,1,4]{2,1,0:T(1,128)} %broadcast_in_dim.42), calls=%async_computation.2 | async-start | bytes 16384 | tf_op jit(solution)/shard_map/all_to_all | solution.py:29
  63.5 0.7 fusion.86
  64.7 3.3 %collective-permute-start = (f32[4,64,1,128]{3,1,2,0:T(8,128)}, f32[4,64,1,128]{3,1,2,0:T(8,128)S(1)}, u32[]{:S(2)}, u32[]{:S(2)}) collective-permute-start(f32[4,64,1,128]{3,1,2,0:T(8,128)} %get-tuple-element.35), channel_id=1, source_target_pairs={{0,32},{32,64},{64,96},{96,128},{128,160},{160,192},{192,224},{224... | collective-permute-start | bytes 393224 | tf_op jit(solution)/shard_map/ppermute | solution.py:21
  68.0 1.3 collective-permute-start.1
  69.5 1.1 copy.55
  70.5 3.3 %collective-permute-done.1 = f32[4,64,1,128]{3,1,2,0:T(8,128)S(1)} collective-permute-done((f32[4,64,1,128]{3,1,2,0:T(8,128)}, f32[4,64,1,128]{3,1,2,0:T(8,128)S(1)}, u32[]{:S(2)}, u32[]{:S(2)}) %collective-permute-start.1) | collective-permute-done | bytes 131104 | tf_op jit(solution)/shard_map/ppermute | solution.py:22
  73.9 1.8 compare_select_fusion
  76.7 0.8 copy-done
  77.7 0.9 multiply_reduce_fusion.5
  78.6 0.7 broadcast_in_dim.47
  79.3 7.7 %all-to-all-start.4 = ((f32[16,1,4]{2,1,0:T(1,128)}), f32[16,1,4]{2,1,0:T(1,128)S(1)}, u32[]{:S(2)}, u32[]{:S(2)}) async-start(f32[16,1,4]{2,1,0:T(1,128)} %broadcast_in_dim.47), calls=%async_computation.4 | async-start | bytes 16384 | tf_op jit(solution)/shard_map/all_to_all | solution.py:29
  87.0 6.7 %all-to-all-done.4 = f32[16,1,4]{2,1,0:T(1,128)S(1)} async-done(((f32[16,1,4]{2,1,0:T(1,128)}), f32[16,1,4]{2,1,0:T(1,128)S(1)}, u32[]{:S(2)}, u32[]{:S(2)}) %all-to-all-start.4) | async-done | bytes 288 | tf_op jit(solution)/shard_map/all_to_all | solution.py:29
  94.0 9.4 %all_to_all.83 = f32[16,1,4]{2,1,0:T(1,128)S(1)} all-to-all(f32[16,1,4]{2,1,0:T(1,128)S(1)} %broadcast_in_dim.48), channel_id=1, replica_groups=mesh['member'=16,'space'=32] {'member'}, dimensions={0} | all-to-all | bytes 512 | tf_op jit(solution)/shard_map/all_to_all | solution.py:29
  103.6 2.2 collective-permute-start.4
  105.8 1.3 collective-permute-start.5
  107.7 3.8 %collective-permute-done.5 = f32[4,64,1,128]{3,1,2,0:T(8,128)S(1)} collective-permute-done((f32[4,64,1,128]{3,1,2,0:T(8,128)S(1)}, f32[4,64,1,128]{3,1,2,0:T(8,128)S(1)}, u32[]{:S(2)}, u32[]{:S(2)}) %collective-permute-start.5) | collective-permute-done | bytes 131104 | tf_op jit(solution)/shard_map/ppermute | solution.py:22
  112.0 1.4 multiply_reduce_fusion.3
  113.5 12.4 %all_to_all.84 = f32[16,1,4]{2,1,0:T(1,128)S(1)} all-to-all(f32[16,1,4]{2,1,0:T(1,128)S(1)} %broadcast_in_dim.49), channel_id=1, replica_groups=mesh['member'=16,'space'=32] {'member'}, dimensions={0} | all-to-all | bytes 512 | tf_op jit(solution)/shard_map/all_to_all | solution.py:29
  125.9 1.3 multiply_reduce_fusion.2
  127.2 9.4 %all_to_all.85 = f32[16,1,4]{2,1,0:T(1,128)S(1)} all-to-all(f32[16,1,4]{2,1,0:T(1,128)S(1)} %broadcast_in_dim.50), channel_id=1, replica_groups=mesh['member'=16,'space'=32] {'member'}, dimensions={0} | all-to-all | bytes 512 | tf_op jit(solution)/shard_map/all_to_all | solution.py:29
  136.8 0.7 fusion.83
  137.5 2.8 collective-permute-start.6
  140.4 1.3 collective-permute-start.7
  142.9 17.0 %all-to-all-start = ((s32[32,1,1,1]{3,2,1,0:T(1,128)}), s32[32,1,1,1]{3,2,1,0:T(1,128)S(1)}, u32[]{:S(2)}, u32[]{:S(2)}) async-start(s32[32,1,1,1]{3,2,1,0:T(1,128)} %broadcast_in_dim.39), calls=%async_computation | async-start | bytes 32768 | tf_op jit(solution)/shard_map/all_to_all | solution.py:29
  159.9 1.2 reduce_sum.179
  161.2 1.5 select_maximum_fusion.2
  162.7 2.4 multiply_reduce_fusion.1
  165.1 6.5 %all-to-all-done = s32[32,1,1,1]{3,2,1,0:T(1,128)S(1)} async-done(((s32[32,1,1,1]{3,2,1,0:T(1,128)}), s32[32,1,1,1]{3,2,1,0:T(1,128)S(1)}, u32[]{:S(2)}, u32[]{:S(2)}) %all-to-all-start) | async-done | bytes 160 | tf_op jit(solution)/shard_map/all_to_all | solution.py:29
  172.2 5.2 %all-to-all-start.8 = ((f32[16,1,4]{2,1,0:T(1,128)}), f32[16,1,4]{2,1,0:T(1,128)S(1)}, u32[]{:S(2)}, u32[]{:S(2)}) async-start(f32[16,1,4]{2,1,0:T(1,128)} %broadcast_in_dim.51), calls=%async_computation.8 | async-start | bytes 16384 | tf_op jit(solution)/shard_map/all_to_all | solution.py:29
  177.5 2.0 reshape.446
  179.5 0.7 reduce.20
  180.2 4.0 %all-to-all-done.8 = f32[16,1,4]{2,1,0:T(1,128)S(1)} async-done(((f32[16,1,4]{2,1,0:T(1,128)}), f32[16,1,4]{2,1,0:T(1,128)S(1)}, u32[]{:S(2)}, u32[]{:S(2)}) %all-to-all-start.8) | async-done | bytes 288 | tf_op jit(solution)/shard_map/all_to_all | solution.py:29
  184.2 1.3 multiply_reduce_fusion
  186.1 3.5 %all-to-all-start.9 = ((f32[16,1,4]{2,1,0:T(1,128)}), f32[16,1,4]{2,1,0:T(1,128)S(1)}, u32[]{:S(2)}, u32[]{:S(2)}) async-start(f32[16,1,4]{2,1,0:T(1,128)} %broadcast_in_dim.52), calls=%async_computation.9 | async-start | bytes 16384 | tf_op jit(solution)/shard_map/all_to_all | solution.py:29
  189.6 6.7 %all-to-all-done.9 = f32[16,1,4]{2,1,0:T(1,128)S(1)} async-done(((f32[16,1,4]{2,1,0:T(1,128)}), f32[16,1,4]{2,1,0:T(1,128)S(1)}, u32[]{:S(2)}, u32[]{:S(2)}) %all-to-all-start.9) | async-done | bytes 288 | tf_op jit(solution)/shard_map/all_to_all | solution.py:29
  196.3 1.4 multiply_add_fusion.1
  197.7 2.3 collective-permute-start.8
  200.1 1.3 collective-permute-start.9
  202.0 3.8 %collective-permute-done.9 = f32[4,64,1,128]{3,1,2,0:T(8,128)S(1)} collective-permute-done((f32[4,64,1,128]{3,1,2,0:T(8,128)S(1)}, f32[4,64,1,128]{3,1,2,0:T(8,128)S(1)}, u32[]{:S(2)}, u32[]{:S(2)}) %collective-permute-start.9) | collective-permute-done | bytes 131104 | tf_op jit(solution)/shard_map/ppermute | solution.py:22
  206.3 0.7 fusion.14
  207.6 5.8 %all-to-all-start.10 = ((f32[16,1,4]{2,1,0:T(1,128)}), f32[16,1,4]{2,1,0:T(1,128)S(1)}, u32[]{:S(2)}, u32[]{:S(2)}) async-start(f32[16,1,4]{2,1,0:T(1,128)} %broadcast_in_dim.53), calls=%async_computation.10 | async-start | bytes 16384 | tf_op jit(solution)/shard_map/all_to_all | solution.py:29
  213.5 6.7 %all-to-all-done.10 = f32[16,1,4]{2,1,0:T(1,128)S(1)} async-done(((f32[16,1,4]{2,1,0:T(1,128)}), f32[16,1,4]{2,1,0:T(1,128)S(1)}, u32[]{:S(2)}, u32[]{:S(2)}) %all-to-all-start.10) | async-done | bytes 288 | tf_op jit(solution)/shard_map/all_to_all | solution.py:29
  221.5 0.7 select_bitcast_fusion
  222.2 11.1 %all-to-all-start.11 = ((f32[4,32,128]{2,0,1:T(4,128)}), f32[4,32,128]{2,0,1:T(4,128)S(1)}, u32[]{:S(2)}, u32[]{:S(2)}) async-start(f32[4,32,128]{2,0,1:T(4,128)} %select_bitcast_fusion), calls=%async_computation.11 | async-start | bytes 131072 | tf_op jit(solution)/shard_map/all_to_all | solution.py:237
  233.4 11.8 %all-to-all-done.11 = f32[4,32,128]{2,0,1:T(4,128)S(1)} async-done(((f32[4,32,128]{2,0,1:T(4,128)}), f32[4,32,128]{2,0,1:T(4,128)S(1)}, u32[]{:S(2)}, u32[]{:S(2)}) %all-to-all-start.11) | async-done | bytes 65568 | tf_op jit(solution)/shard_map/all_to_all | solution.py:237
  245.9 0.7 pad_maximum_fusion.14
  246.6 27.9 %sum_everywhere.1 = f32[64,4,128]{2,1,0:T(4,128)} custom-call(f32[64,4,128]{2,1,0:T(4,128)} %bitcast.95), custom_call_target="tpu_custom_call" | custom-call | tf_op jit(solution)/shard_map/sum_everywhere/pallas_call | solution.py:138
  274.5 0.9 fusion.87
  275.6 11.7 %cholesky.16 = f32[128,128]{1,0:T(8,128)S(1)} custom-call(f32[128,128]{1,0:T(8,128)S(1)} %fusion.72), custom_call_target="Cholesky" | custom-call | tf_op jit(solution)/shard_map/jit(cholesky)/cholesky | solution.py:247
  287.3 0.6 compare_reduce_fusion
  288.0 0.7 fusion.67
  288.6 9.8 %custom-call.10 = f32[1,128,128]{1,2,0:T(8,128)S(1)} custom-call(f32[1,128,128]{2,1,0:T(8,128)S(1)} %fusion.67), custom_call_target="InvertDiagBlocksLowerTriangular" | custom-call | tf_op jit(solution)/shard_map/jit(_cho_solve)/triangular_solve | solution.py:250
  299.0 0.6 convolution_add_fusion
  299.6 1.0 reshape.450
  (101 shorter events, 11.8 us)
Async XLA Ops:
  30.5 22.4 %all-to-all-start.3 = ((f32[128,2,4,128]{3,2,1,0:T(4,128)}), f32[128,2,4,128]{3,2,1,0:T(4,128)S(1)}, u32[]{:S(2)}, u32[]{:S(2)}) async-start(f32[128,2,4,128]{3,2,1,0:T(4,128)} %param.6), calls=%async_computation.3 | async-start | bytes 1048576 | tf_op jit(solution)/shard_map/all_to_all | solution.py:227
  35.2 5.6 %collective-permute-start.2 = (f32[4,64,1,128]{3,1,2,0:T(8,128)S(1)}, f32[4,64,1,128]{3,1,2,0:T(8,128)S(1)}, u32[]{:S(2)}, u32[]{:S(2)}) collective-permute-start(f32[4,64,1,128]{3,1,2,0:T(8,128)S(1)} %broadcast_in_dim.45), channel_id=1, source_target_pairs={{0,32},{32,64},{64,96},{96,128},{128,160},{160,192},{192,224},{224... | collective-permute-start | bytes 393224 | tf_op jit(solution)/shard_map/ppermute | solution.py:21
  38.4 6.3 %collective-permute-start.3 = (f32[4,64,1,128]{3,1,2,0:T(8,128)S(1)}, f32[4,64,1,128]{3,1,2,0:T(8,128)S(1)}, u32[]{:S(2)}, u32[]{:S(2)}) collective-permute-start(f32[4,64,1,128]{3,1,2,0:T(8,128)S(1)} %broadcast_in_dim.46), channel_id=1, source_target_pairs={{32,0},{64,32},{96,64},{128,96},{160,128},{192,160},{224,192},{256... | collective-permute-start | bytes 393224 | tf_op jit(solution)/shard_map/ppermute | solution.py:22
  40.9 13.2 %copy-start.7 = (f32[4,64,1,128]{3,1,2,0:T(8,128)}, f32[4,64,1,128]{3,1,2,0:T(8,128)S(1)}, u32[]{:S(2)}) copy-start(f32[4,64,1,128]{3,1,2,0:T(8,128)S(1)} %collective-permute-done.2) | copy-start | bytes 393220
  44.7 9.3 %copy-start.9 = (f32[4,64,1,128]{3,1,2,0:T(8,128)}, f32[4,64,1,128]{3,1,2,0:T(8,128)S(1)}, u32[]{:S(2)}) copy-start(f32[4,64,1,128]{3,1,2,0:T(8,128)S(1)} %collective-permute-done.3) | copy-start | bytes 393220
  54.1 24.6 %all-to-all-start.2 = ((f32[16,1,4]{2,1,0:T(1,128)}), f32[16,1,4]{2,1,0:T(1,128)S(1)}, u32[]{:S(2)}, u32[]{:S(2)}) async-start(f32[16,1,4]{2,1,0:T(1,128)} %broadcast_in_dim.42), calls=%async_computation.2 | async-start | bytes 16384 | tf_op jit(solution)/shard_map/all_to_all | solution.py:29
  64.7 5.9 %collective-permute-start = (f32[4,64,1,128]{3,1,2,0:T(8,128)}, f32[4,64,1,128]{3,1,2,0:T(8,128)S(1)}, u32[]{:S(2)}, u32[]{:S(2)}) collective-permute-start(f32[4,64,1,128]{3,1,2,0:T(8,128)} %get-tuple-element.35), channel_id=1, source_target_pairs={{0,32},{32,64},{64,96},{96,128},{128,160},{160,192},{192,224},{224... | collective-permute-start | bytes 393224 | tf_op jit(solution)/shard_map/ppermute | solution.py:21
  68.0 5.9 %collective-permute-start.1 = (f32[4,64,1,128]{3,1,2,0:T(8,128)}, f32[4,64,1,128]{3,1,2,0:T(8,128)S(1)}, u32[]{:S(2)}, u32[]{:S(2)}) collective-permute-start(f32[4,64,1,128]{3,1,2,0:T(8,128)} %get-tuple-element.36), channel_id=1, source_target_pairs={{32,0},{64,32},{96,64},{128,96},{160,128},{192,160},{224,192},{256... | collective-permute-start | bytes 393224 | tf_op jit(solution)/shard_map/ppermute | solution.py:22
  76.1 1.5 copy-start
  76.1 1.6 copy-start.6
  76.1 1.6 copy-start.8
  76.1 1.6 copy-start.10
  78.6 33.4 %copy-start.2 = (f32[4,64,4,128]{3,1,2,0:T(8,128)}, f32[4,64,4,128]{3,1,2,0:T(8,128)S(1)}, u32[]{:S(2)}) copy-start(f32[4,64,4,128]{3,1,2,0:T(8,128)S(1)} %get-tuple-element.22) | copy-start | bytes 1572868
  79.3 14.4 %all-to-all-start.4 = ((f32[16,1,4]{2,1,0:T(1,128)}), f32[16,1,4]{2,1,0:T(1,128)S(1)}, u32[]{:S(2)}, u32[]{:S(2)}) async-start(f32[16,1,4]{2,1,0:T(1,128)} %broadcast_in_dim.47), calls=%async_computation.4 | async-start | bytes 16384 | tf_op jit(solution)/shard_map/all_to_all | solution.py:29
  103.6 4.1 %collective-permute-start.4 = (f32[4,64,1,128]{3,1,2,0:T(8,128)S(1)}, f32[4,64,1,128]{3,1,2,0:T(8,128)S(1)}, u32[]{:S(2)}, u32[]{:S(2)}) collective-permute-start(f32[4,64,1,128]{3,1,2,0:T(8,128)S(1)} %get-tuple-element.31), channel_id=1, source_target_pairs={{0,32},{32,64},{64,96},{96,128},{128,160},{160,192},{192,224},{224... | collective-permute-start | bytes 393224 | tf_op jit(solution)/shard_map/ppermute | solution.py:21
  105.8 5.7 %collective-permute-start.5 = (f32[4,64,1,128]{3,1,2,0:T(8,128)S(1)}, f32[4,64,1,128]{3,1,2,0:T(8,128)S(1)}, u32[]{:S(2)}, u32[]{:S(2)}) collective-permute-start(f32[4,64,1,128]{3,1,2,0:T(8,128)S(1)} %get-tuple-element.32), channel_id=1, source_target_pairs={{32,0},{64,32},{96,64},{128,96},{160,128},{192,160},{224,192},{256... | collective-permute-start | bytes 393224 | tf_op jit(solution)/shard_map/ppermute | solution.py:22
  127.2 57.0 %copy-start.1 = (f32[4,64,4,128]{3,1,2,0:T(8,128)}, f32[4,64,4,128]{3,1,2,0:T(8,128)S(1)}, u32[]{:S(2)}) copy-start(f32[4,64,4,128]{3,1,2,0:T(8,128)S(1)} %get-tuple-element.17) | copy-start | bytes 1572868
  137.5 23.6 %collective-permute-start.6 = (f32[4,64,1,128]{3,1,2,0:T(8,128)}, f32[4,64,1,128]{3,1,2,0:T(8,128)}, u32[]{:S(2)}, u32[]{:S(2)}) collective-permute-start(f32[4,64,1,128]{3,1,2,0:T(8,128)} %get-tuple-element.29), channel_id=1, source_target_pairs={{0,32},{32,64},{64,96},{96,128},{128,160},{160,192},{192,224},{224... | collective-permute-start | bytes 393224 | tf_op jit(solution)/shard_map/ppermute | solution.py:21
  140.4 20.8 %collective-permute-start.7 = (f32[4,64,1,128]{3,1,2,0:T(8,128)}, f32[4,64,1,128]{3,1,2,0:T(8,128)}, u32[]{:S(2)}, u32[]{:S(2)}) collective-permute-start(f32[4,64,1,128]{3,1,2,0:T(8,128)} %get-tuple-element.30), channel_id=1, source_target_pairs={{32,0},{64,32},{96,64},{128,96},{160,128},{192,160},{224,192},{256... | collective-permute-start | bytes 393224 | tf_op jit(solution)/shard_map/ppermute | solution.py:22
  142.9 28.7 %all-to-all-start = ((s32[32,1,1,1]{3,2,1,0:T(1,128)}), s32[32,1,1,1]{3,2,1,0:T(1,128)S(1)}, u32[]{:S(2)}, u32[]{:S(2)}) async-start(s32[32,1,1,1]{3,2,1,0:T(1,128)} %broadcast_in_dim.39), calls=%async_computation | async-start | bytes 32768 | tf_op jit(solution)/shard_map/all_to_all | solution.py:29
  161.1 1.6 copy-start.3
  172.2 11.9 %all-to-all-start.8 = ((f32[16,1,4]{2,1,0:T(1,128)}), f32[16,1,4]{2,1,0:T(1,128)S(1)}, u32[]{:S(2)}, u32[]{:S(2)}) async-start(f32[16,1,4]{2,1,0:T(1,128)} %broadcast_in_dim.51), calls=%async_computation.8 | async-start | bytes 16384 | tf_op jit(solution)/shard_map/all_to_all | solution.py:29
  186.1 10.2 %all-to-all-start.9 = ((f32[16,1,4]{2,1,0:T(1,128)}), f32[16,1,4]{2,1,0:T(1,128)S(1)}, u32[]{:S(2)}, u32[]{:S(2)}) async-start(f32[16,1,4]{2,1,0:T(1,128)} %broadcast_in_dim.52), calls=%async_computation.9 | async-start | bytes 16384 | tf_op jit(solution)/shard_map/all_to_all | solution.py:29
  197.7 8.6 %copy-start.4 = (f32[4,64,4,128]{3,1,2,0:T(8,128)S(1)}, f32[4,64,4,128]{3,1,2,0:T(8,128)}, u32[]{:S(2)}) copy-start(f32[4,64,4,128]{3,1,2,0:T(8,128)} %copy-done.2) | copy-start | bytes 1572868
  197.7 4.3 %collective-permute-start.8 = (f32[4,64,1,128]{3,1,2,0:T(8,128)S(1)}, f32[4,64,1,128]{3,1,2,0:T(8,128)S(1)}, u32[]{:S(2)}, u32[]{:S(2)}) collective-permute-start(f32[4,64,1,128]{3,1,2,0:T(8,128)S(1)} %get-tuple-element.27), channel_id=1, source_target_pairs={{0,32},{32,64},{64,96},{96,128},{128,160},{160,192},{192,224},{224... | collective-permute-start | bytes 393224 | tf_op jit(solution)/shard_map/ppermute | solution.py:21
  200.1 5.7 %collective-permute-start.9 = (f32[4,64,1,128]{3,1,2,0:T(8,128)S(1)}, f32[4,64,1,128]{3,1,2,0:T(8,128)S(1)}, u32[]{:S(2)}, u32[]{:S(2)}) collective-permute-start(f32[4,64,1,128]{3,1,2,0:T(8,128)S(1)} %get-tuple-element.28), channel_id=1, source_target_pairs={{32,0},{64,32},{96,64},{128,96},{160,128},{192,160},{224,192},{256... | collective-permute-start | bytes 393224 | tf_op jit(solution)/shard_map/ppermute | solution.py:22
  207.6 12.6 %all-to-all-start.10 = ((f32[16,1,4]{2,1,0:T(1,128)}), f32[16,1,4]{2,1,0:T(1,128)S(1)}, u32[]{:S(2)}, u32[]{:S(2)}) async-start(f32[16,1,4]{2,1,0:T(1,128)} %broadcast_in_dim.53), calls=%async_computation.10 | async-start | bytes 16384 | tf_op jit(solution)/shard_map/all_to_all | solution.py:29
  220.2 13.2 %copy-start.13 = (f32[1,1,128]{2,1,0:T(1,128)S(1)}, f32[1,1,128]{2,1,0:T(1,128)}, u32[]{:S(2)}) copy-start(f32[1,1,128]{2,1,0:T(1,128)} %param.11) | copy-start | bytes 1540
  220.2 25.3 %copy-start.11 = (f32[128,1,1,128]{3,2,1,0:T(1,128)S(1)}, f32[128,1,1,128]{3,2,1,0:T(1,128)}, u32[]{:S(2)}) copy-start(f32[128,1,1,128]{3,2,1,0:T(1,128)} %param.10) | copy-start | bytes 196612
  220.3 25.3 %copy-start.12 = (f32[1,1,128]{2,1,0:T(1,128)S(1)}, f32[1,1,128]{2,1,0:T(1,128)}, u32[]{:S(2)}) copy-start(f32[1,1,128]{2,1,0:T(1,128)} %param.9) | copy-start | bytes 1540
  220.9 78.1 %copy-start.5 = (f32[128,1024]{1,0:T(8,128)S(1)}, f32[128,1024]{1,0:T(8,128)}, u32[]{:S(2)}) copy-start(f32[128,1024]{1,0:T(8,128)} %reshape.446) | copy-start | bytes 1572868
  222.2 23.0 %all-to-all-start.11 = ((f32[4,32,128]{2,0,1:T(4,128)}), f32[4,32,128]{2,0,1:T(4,128)S(1)}, u32[]{:S(2)}, u32[]{:S(2)}) async-start(f32[4,32,128]{2,0,1:T(4,128)} %select_bitcast_fusion), calls=%async_computation.11 | async-start | bytes 131072 | tf_op jit(solution)/shard_map/all_to_all | solution.py:237

commit v2 on v1

--- a/solution.py
+++ b/solution.py
@@ -11,27 +11,9 @@
 ITERS = 4
 
 
-def padded_2(x, sides, width):
-    for axis, dim in sides:
-        devices, length = (lax.axis_size(axis), x.shape[dim])
-        up = [(i, (i + 1) % devices) for i in range(devices - 1)]
-        down = [(j, i) for i, j in up]
-        last = lax.slice_in_dim(x, length - width, length, axis=dim)
-        leading = lax.slice_in_dim(x, 0, width, axis=dim)
-        before = lax.ppermute(last, axis, up)
-        after = lax.ppermute(leading, axis, down)
-        x = jnp.concatenate([before, x, after], axis=dim)
-    return x
-
-
 def from_everyone(x, axis):
     devices = lax.axis_size(axis)
     return lax.all_to_all(jnp.broadcast_to(x[None], (devices, *x.shape)), axis, 0, 0, tiled=True)
-
-
-def over_copies(x, axis):
-    everything = from_everyone(x, axis)
-    return jnp.sum(everything, axis=0)
 
 
 def joined_along(pieces, dim):
@@ -160,81 +142,330 @@
     return 2.0 * first_cond * second_cond / (first_cond + second_cond)
 
 
-def extend_cond(cond):
-    widened = padded_2(cond, (("member", 2),), 1)
-    return jnp.pad(widened, ((0, 0), (1, 1), (0, 0), (1, 1)))
-
-
-def extend_values(values_in):
-    widened = padded_2(values_in, (("member", 2),), 1)
-    return jnp.pad(widened, ((0, 0), (1, 1), (0, 0), (1, 1)))
-
-
-def member_dots(dot_terms):
-    return over_copies(dot_terms, "member")
-
-
-def face_terms(cond):
-    widened = extend_cond(cond)
-    edge_pad = jnp.pad(cond, ((0, 0), (1, 1), (1, 1), (1, 1)), mode="edge")
-    cond_pad = jnp.where(widened > 0.0, widened, edge_pad)
-    face_x = harmonic(cond_pad[:, :-1, 1:-1, 1:-1], cond_pad[:, 1:, 1:-1, 1:-1])
-    face_y = harmonic(cond_pad[:, 1:-1, :-1, 1:-1], cond_pad[:, 1:-1, 1:, 1:-1])
-    face_z = harmonic(cond, cond_pad[:, 1:-1, 1:-1, 2:])
-    lower_z = jnp.concatenate([harmonic(cond[..., :1], cond[..., :1]), face_z[..., :-1]], axis=-1)
-    return (face_x, face_y, face_z, lower_z)
-
-
-def operate(values_in, face_x, face_y, face_z, lower_z):
-    padded = extend_values(values_in)
-    result = face_x[:, 1:] * (values_in - padded[:, 2:, 1:-1, 1:-1]) + face_x[:, :-1] * (
-        values_in - padded[:, :-2, 1:-1, 1:-1]
-    )
-    result = (
-        result
-        + face_y[:, :, 1:] * (values_in - padded[:, 1:-1, 2:, 1:-1])
-        + face_y[:, :, :-1] * (values_in - padded[:, 1:-1, :-2, 1:-1])
-    )
-    result = (
-        result
-        + face_z * (values_in - padded[:, 1:-1, 1:-1, 2:])
-        + lower_z * (values_in - padded[:, 1:-1, 1:-1, :-2])
-    )
-    return result
-
-
-def conjugate(cond, forcing):
-    face_x, face_y, face_z, lower_z = face_terms(cond)
-    residual = jnp.broadcast_to(forcing[None], cond.shape)
-    direction = residual
-    solution = jnp.zeros_like(cond)
-    norm_now = member_dots(jnp.sum(residual * residual, axis=(1, 2, 3)))
-    for iteration in range(ITERS):
-        image = operate(direction, face_x, face_y, face_z, lower_z)
-        step_size = norm_now / member_dots(jnp.sum(direction * image, axis=(1, 2, 3)))
-        solution = solution + step_size[:, None, None, None] * direction
-        residual = residual - step_size[:, None, None, None] * image
-        if iteration + 1 < ITERS:
-            norm_next = member_dots(jnp.sum(residual * residual, axis=(1, 2, 3)))
-            direction = residual + (norm_next / norm_now)[:, None, None, None] * direction
-            norm_now = norm_next
-    return solution
+HALF = 32
+TEAM = 16
+COND, SOURCE = ITERS - 1, ITERS
+
+
+def conjugate_kernel(
+    field,
+    source,
+    wanted,
+    picked,
+    cond,
+    face_x,
+    face_y,
+    face_z,
+    lower_z,
+    searched,
+    image,
+    residual,
+    direction,
+    along,
+    beyond,
+    answer,
+    cond_edge,
+    source_edge,
+    edges,
+    tiles,
+    edge_send,
+    edge_recv,
+    tile_send,
+    tile_recv,
+):
+    member = lax.axis_index("member")
+    plane = (8, 128)
+    sublane = lax.broadcasted_iota(jnp.int32, plane, 0)
+    lane = lax.broadcasted_iota(jnp.int32, plane, 1)
+    lane_4 = lax.broadcasted_iota(jnp.int32, (4, 8, 128), 2)
+    low_half = sublane < 4
+
+    def team_peer(step):
+        return {"member": lax.rem(member + step, TEAM)}
+
+    def edge_copy(kind, upward):
+        if kind == COND:
+            origin, target = field.at[3 * upward], cond_edge.at[1 - upward]
+        elif kind == SOURCE:
+            origin, target = source.at[3 * upward], source_edge.at[1 - upward]
+        else:
+            origin, target = searched.at[3 * upward, pl.ds(1, HALF)], edges.at[kind, 1 - upward]
+        return pltpu.make_async_remote_copy(
+            src_ref=origin,
+            dst_ref=target,
+            send_sem=edge_send.at[kind, upward],
+            recv_sem=edge_recv.at[kind, 1 - upward],
+            device_id=team_peer(1 if upward else TEAM - 1),
+            device_id_type=pl.DeviceIdType.MESH,
+        )
+
+    def send_edges(kind):
+        @pl.when(member > 0)
+        def _():
+            edge_copy(kind, 0).start()
+
+        @pl.when(member < TEAM - 1)
+        def _():
+            edge_copy(kind, 1).start()
+
+    def edges_sent(kind):
+        @pl.when(member > 0)
+        def _():
+            edge_copy(kind, 0).wait_send()
+
+        @pl.when(member < TEAM - 1)
+        def _():
+            edge_copy(kind, 1).wait_send()
+
+    def edges_here(kind):
+        @pl.when(member > 0)
+        def _():
+            edge_copy(kind, 1).wait_recv()
+
+        @pl.when(member < TEAM - 1)
+        def _():
+            edge_copy(kind, 0).wait_recv()
+
+    def tile_copy(turn, step):
+        return pltpu.make_async_remote_copy(
+            src_ref=tiles.at[turn, member],
+            dst_ref=tiles.at[turn, member],
+            send_sem=tile_send.at[turn, step - 1],
+            recv_sem=tile_recv.at[turn, step - 1],
+            device_id=team_peer(step),
+            device_id_type=pl.DeviceIdType.MESH,
+        )
+
+    def send_sums(turn, norm, product):
+        norm = norm + pltpu.roll(norm, 64, 1)
+        product = product + pltpu.roll(product, 64, 1)
+        tiles[turn, member] = jnp.where(lane < 64, norm, product)
+        for step in range(1, TEAM):
+            tile_copy(turn, step).start()
+
+    def sums_here(turn):
+        for step in range(1, TEAM):
+            tile_copy(turn, step).wait_recv()
+        both = jnp.sum(tiles[turn], axis=0)
+        both = both + pltpu.roll(both, 4, 0)
+        norm = jnp.sum(jnp.where(lane < 64, both, 0.0), axis=1, keepdims=True)
+        product = jnp.sum(jnp.where(lane < 64, 0.0, both), axis=1, keepdims=True)
+        return jnp.broadcast_to(norm, plane), jnp.broadcast_to(product, plane)
+
+    def over_rows(body, start, width=2):
+        def several(block, carry):
+            for k in range(width):
+                carry = body(block * width + k, carry)
+            return carry
+
+        return lax.fori_loop(0, HALF // width, several, start)
+
+    barrier = pltpu.get_barrier_semaphore()
+    for step in range(1, TEAM):
+        pl.semaphore_signal(barrier, inc=1, device_id=team_peer(step), device_id_type=pl.DeviceIdType.MESH)
+    pl.semaphore_wait(barrier, TEAM - 1)
+    send_edges(COND)
+    send_edges(SOURCE)
+
+    @pl.when(member == 0)
+    def _():
+        cond_edge[0] = field[0]
+        source_edge[0] = jnp.zeros(source_edge.shape[1:], jnp.float32)
+        for kind in range(ITERS - 1):
+            edges[kind, 0] = jnp.zeros(edges.shape[2:], jnp.float32)
+
+    @pl.when(member == TEAM - 1)
+    def _():
+        cond_edge[1] = field[3]
+        source_edge[1] = jnp.zeros(source_edge.shape[1:], jnp.float32)
+        for kind in range(ITERS - 1):
+            edges[kind, 1] = jnp.zeros(edges.shape[2:], jnp.float32)
+
+    def spread_source(rows):
+        lower, upper = rows[..., 0:1, :], rows[..., 1:2, :]
+        shape = (*rows.shape[:-2], *plane)
+        return jnp.where(low_half, jnp.broadcast_to(lower, shape), jnp.broadcast_to(upper, shape))
+
+    def close_ends(padded, outside):
+        for y in range(4):
+            first, last = padded[y, 1], padded[y, HALF]
+            below = first if outside is None else outside
+            above = last if outside is None else outside
+            padded[y, 0] = jnp.where(low_half, below, pltpu.roll(last, 4, 0))
+            padded[y, HALF + 1] = jnp.where(low_half, pltpu.roll(first, 4, 0), above)
+
+    def begin(row, carry):
+        cond[:, row + 1] = jnp.exp(field[:, row])
+        searched[:, row + 1] = spread_source(source[:, row])
+        return carry
+
+    over_rows(begin, 0)
+    close_ends(cond, None)
+    close_ends(searched, jnp.zeros(plane, jnp.float32))
+
+    def inner_faces(row, carry):
+        here = cond[:, row + 1]
+        face_x[:, row + 1] = harmonic(here, cond[:, row + 2])
+        above = jnp.where(lane_4 == 127, here, pltpu.roll(here, 127, 2))
+        upper = harmonic(here, above)
+        face_z[:, row] = upper
+        lower_z[:, row] = jnp.where(lane_4 == 0, here, pltpu.roll(upper, 1, 2))
+        face_y[1:4, row] = harmonic(here[:3], here[1:])
+        return carry
+
+    over_rows(inner_faces, 0)
+    for y in range(4):
+        face_x[y, 0] = harmonic(cond[y, 0], cond[y, 1])
+    edges_here(COND)
+
+    def outer_faces(row, carry):
+        face_y[0, row] = harmonic(jnp.exp(cond_edge[0, row]), cond[0, row + 1])
+        face_y[4, row] = harmonic(cond[3, row + 1], jnp.exp(cond_edge[1, row]))
+        return carry
+
+    over_rows(outer_faces, 0)
+
+    def operate(lower_edge, upper_edge):
+        def body(row, carry):
+            here = searched[:, row + 1]
+            before = jnp.concatenate([lower_edge(row)[None], here[:3]])
+            after = jnp.concatenate([here[1:], upper_edge(row)[None]])
+            result = face_x[:, row + 1] * (here - searched[:, row + 2])
+            result = result + face_x[:, row] * (here - searched[:, row])
+            result = result + face_y[1:5, row] * (here - after)
+            result = result + face_y[0:4, row] * (here - before)
+            above = jnp.where(lane_4 == 127, 0.0, pltpu.roll(here, 127, 2))
+            below = jnp.where(lane_4 == 0, 0.0, pltpu.roll(here, 1, 2))
+            result = result + face_z[:, row] * (here - above)
+            image[:, row] = result + lower_z[:, row] * (here - below)
+            return carry
+
+        over_rows(body, 0)
+
+    zeros = jnp.zeros(plane, jnp.float32)
+    edges_here(SOURCE)
+    operate(lambda row: spread_source(source_edge[0, row]), lambda row: spread_source(source_edge[1, row]))
+
+    def first_sums(row, carry):
+        norm, product = carry
+        image_here = image[:, row]
+        residual_here = searched[:, row + 1]
+        residual[:, row] = residual_here
+        searched[:, row + 1] = image_here
+        return norm + jnp.sum(residual_here * residual_here, axis=0), product + jnp.sum(
+            residual_here * image_here, axis=0
+        )
+
+    norm, product = over_rows(first_sums, (zeros, zeros))
+
+    norm_before = step_before = None
+    for turn in range(ITERS):
+        last = turn == ITERS - 1
+        send_sums(turn, norm, product)
+        if not last:
+            send_edges(turn)
+            close_ends(searched, zeros)
+            edges_here(turn)
+            operate(lambda row: edges[turn, 0, row], lambda row: edges[turn, 1, row])
+        norm_now, product_now = sums_here(turn)
+        if turn == 0:
+            step_size = norm_now / product_now
+        else:
+            ratio = norm_now / norm_before
+            step_size = norm_now / (product_now - ratio * norm_now / step_before)
+        norm_before, step_before = norm_now, step_size
+
+        def update(row, carry):
+            norm, product = carry
+            residual_here, image_here = residual[:, row], searched[:, row + 1]
+            direction_here, along_here, beyond_here = residual_here, image_here, image[:, row]
+            answer_here = step_size * direction_here
+            if turn > 0:
+                direction_here = direction_here + ratio * direction[:, row]
+                along_here = along_here + ratio * along[:, row]
+                beyond_here = beyond_here + ratio * beyond[:, row]
+                answer_here = answer[:, row] + step_size * direction_here
+            residual_here = residual_here - step_size * along_here
+            image_here = image_here - step_size * beyond_here
+            answer[:, row] = answer_here
+            direction[:, row] = direction_here
+            along[:, row] = along_here
+            beyond[:, row] = beyond_here
+            residual[:, row] = residual_here
+            searched[:, row + 1] = image_here
+            return norm + jnp.sum(residual_here * residual_here, axis=0), product + jnp.sum(
+                residual_here * image_here, axis=0
+            )
+
+        def finish(row, carry):
+            answer[:, row] = answer[:, row] + step_size * (residual[:, row] + ratio * direction[:, row])
+            return carry
+
+        if last:
+            over_rows(finish, 0)
+        else:
+            edges_sent(turn)
+            norm, product = over_rows(update, (zeros, zeros))
+
+    for block in range(HALF // 2):
+        chosen = wanted[block]
+        value = zeros
+        for choice in range(8):
+            value = value + jnp.where(chosen == choice, answer[choice % 4, 2 * block + choice // 4], 0.0)
+        picked[block] = value[:4]
+        picked[HALF // 2 + block] = value[4:]
+
+    edges_sent(COND)
+    edges_sent(SOURCE)
+    for turn in range(ITERS):
+        for step in range(1, TEAM):
+            tile_copy(turn, step).wait_send()
+
+
+def observed_pressure(field, source, wanted):
+    held = field.shape
+    padded = (held[0], held[1] + 2, *held[2:])
+    edge = held[1:]
+    vmem = lambda *shape: pltpu.VMEM(shape, jnp.float32)
+    return pl.pallas_call(
+        conjugate_kernel,
+        out_shape=jax.ShapeDtypeStruct((HALF, 4, 128), jnp.float32),
+        in_specs=[pl.BlockSpec(memory_space=pltpu.VMEM)] * 3,
+        out_specs=pl.BlockSpec(memory_space=pltpu.VMEM),
+        scratch_shapes=[
+            vmem(*padded),
+            vmem(held[0], held[1] + 1, *held[2:]),
+            vmem(held[0] + 1, *held[1:]),
+            vmem(*held),
+            vmem(*held),
+            vmem(*padded),
+            *[vmem(*held)] * 6,
+            vmem(2, *edge),
+            vmem(2, *source.shape[1:]),
+            vmem(ITERS - 1, 2, *edge),
+            vmem(ITERS, TEAM, *held[2:]),
+            pltpu.SemaphoreType.DMA((ITERS + 1, 2)),
+            pltpu.SemaphoreType.DMA((ITERS + 1, 2)),
+            pltpu.SemaphoreType.DMA((ITERS, TEAM - 1)),
+            pltpu.SemaphoreType.DMA((ITERS, TEAM - 1)),
+        ],
+        compiler_params=pltpu.CompilerParams(collective_id=2, has_side_effects=True),
+        name="observed_pressure",
+    )(field, source, wanted)
 
 
 def local(ensemble, source, obs_rows, obs_values, obs_noise, obs_var):
     total_members = ensemble.shape[0]
     block_x, block_y, layers = source.shape
     held_fields = lax.all_to_all(ensemble, "space", split_axis=0, concat_axis=1, tiled=True)
-    forcing = collect(source, "space", 0)
-    pressure = conjugate(jnp.exp(held_fields), forcing)
-    held_count = pressure.shape[0]
-    cells_flat = pressure.reshape(held_count, -1, layers)
-    gathered_rows = collect(obs_rows, "space", 0)
-    row_ids = gathered_rows[:, 0]
-    peer_ids = jnp.arange(row_ids.shape[0], dtype=jnp.int32)[:, None]
-    flat_index = (peer_ids * block_x + row_ids // block_y) * block_y + row_ids % block_y
-    picked = jnp.take(cells_flat, flat_index.reshape(-1), axis=1)
-    returned = lax.all_to_all(picked, "space", split_axis=1, concat_axis=0, tiled=True)
+    held_count = held_fields.shape[0]
+    field = held_fields.reshape(held_count, 2, HALF, block_y, layers).transpose(3, 2, 1, 0, 4)
+    field = field.reshape(block_y, HALF, 2 * held_count, layers)
+    forcing = collect(source, "space", 0).reshape(2, HALF, block_y, layers).transpose(2, 1, 0, 3)
+    gathered_rows = collect(obs_rows, "space", 0).reshape(2, -1).T
+    wanted = jnp.broadcast_to(gathered_rows[:, :, None, None], (HALF // 2, 2, held_count, layers))
+    picked = observed_pressure(field, forcing, wanted.reshape(HALF // 2, 2 * held_count, layers))
+    returned = lax.all_to_all(picked, "space", split_axis=0, concat_axis=0, tiled=True)
     predicted = returned.reshape(total_members, 1, 1, -1)
     flat_pred = returned.reshape(total_members, -1)
     inv_sigma = 1.0 / jnp.sqrt(obs_var.reshape(-1))

time: 303 us -> 193 us (0.64)
  starting transfers between devices: 84.3 us -> 31.2 us
  blocking collectives: 60.2 us -> 15.5 us
  Pallas kernels: 27.9 us -> 71.3 us
  waiting for transfers between devices: 65.1 us -> 39.1 us
  other arithmetic: 44.9 us -> 24.5 us
  local copies, waits for them, and re-layouts: 15.3 us -> 7.25 us
    all_to_all x4 -> x1, blocking collectives: 60.2 us -> 15.5 us  [from_everyone(): lax.all_to_all(jnp.broadcast_to(x[None], (devices, *x.shape)), axis, 0, 0...]
    pallas_call x0 -> x1, Pallas kernels: none -> 42.7 us  [observed_pressure(): pl.pallas_call(conjugate_kernel, out_shape=jax.ShapeDtypeStruct((HALF, 4,...]
    all_to_all x6 -> x1, starting transfers between devices: 48.2 us -> 17.4 us  [from_everyone(): lax.all_to_all(jnp.broadcast_to(x[None], (devices, *x.shape)), axis, 0, 0...]
    ppermute x10 -> x0, starting transfers between devices: 20.2 us -> none  [the longest x5 13.8 us: padded_2(): before = lax.ppermute(last, axis, up)]
    all_to_all x6 -> x1, waiting for transfers between devices: 30.5 us -> 11.7 us  [from_everyone(): lax.all_to_all(jnp.broadcast_to(x[None], (devices, *x.shape)), axis, 0, 0...]
    ppermute x10 -> x0, waiting for transfers between devices: 16.4 us -> none  [the longest x5 14.8 us: padded_2(): after = lax.ppermute(leading, axis, down)]
    all_to_all x1, waiting for transfers between devices: 6.29 us -> 15.6 us  [local(): lax.all_to_all(ensemble, 'space', split_axis=0, concat_axis=1, tiled=True)]
    reduce_sum x16 -> x0, other arithmetic: 9.29 us -> none  [the longest x4 5.43 us: conjugate(): jnp.sum(direction * image, axis=(1, 2, 3))]
  transfers between devices with their start and end apart: 18 -> 3, of which waited for: 14 -> 3; matrix products, arithmetic and copies ran while one was open for 6% -> 1% of each run, Pallas kernels for 0% -> 0%
where the time goes in v2:
time: 193 us; the launch traced here: 192 us
  Pallas kernels  71.3 us (37%)
  waiting for transfers between devices  39.1 us (20%)
  starting transfers between devices  31.2 us (16%)
  other arithmetic  24.5 us (13%)
  blocking collectives  15.5 us (8%)
  local copies, waits for them, and re-layouts  7.25 us (4%)
    pallas_call x1, Pallas kernels, observed_pressure(): pl.pallas_call(conjugate_kernel, out_shape=jax.ShapeDtypeStruct((HALF, 4,...  42.7 us
    pallas_call x1, Pallas kernels, sum_everywhere(): pl.pallas_call(sum_kernel, out_shape=jax.ShapeDtypeStruct(part.shape, jnp...  28.7 us
    all_to_all x1, starting transfers between devices, from_everyone(): lax.all_to_all(jnp.broadcast_to(x[None], (devices, *x.shape)), axis, 0, 0...  17.4 us
    all_to_all x1, waiting for transfers between devices, local(): lax.all_to_all(ensemble, 'space', split_axis=0, concat_axis=1, tiled=True)  15.6 us
    all_to_all x1, blocking collectives, from_everyone(): lax.all_to_all(jnp.broadcast_to(x[None], (devices, *x.shape)), axis, 0, 0...  15.5 us
    another operation x3, other arithmetic, local(): jnp.linalg.cholesky(gram_sum + (total_members - 1.0) * jnp.eye(total_memb...  12.4 us
    all_to_all x1, waiting for transfers between devices, local(): lax.all_to_all(picked, 'space', split_axis=0, concat_axis=0, tiled=True)  11.8 us
    all_to_all x1, waiting for transfers between devices, from_everyone(): lax.all_to_all(jnp.broadcast_to(x[None], (devices, *x.shape)), axis, 0, 0...  11.7 us
  transfers between devices with their start and end apart: 3, of which 3 were waited for; matrix products, arithmetic and copies ran while one was open for 1% of the time, Pallas kernels for 0%

profile of v2, /device:TPU:1, one launch (start us, length us, event | category | flops | bytes accessed | tf_op | source)
XLA Modules:
  0.0 192.1 jit_solution(3170051017854223296)
XLA Ops:
  1.3 0.6 broadcast_in_dim.15
  1.9 0.0 copy-start.2
  1.9 17.4 %all-to-all-start.2 = ((s32[32,1,1,1]{3,2,1,0:T(1,128)}), s32[32,1,1,1]{3,2,1,0:T(1,128)S(1)}, u32[]{:S(2)}, u32[]{:S(2)}) async-start(s32[32,1,1,1]{3,2,1,0:T(1,128)} %broadcast_in_dim.15), calls=%async_computation.2 | async-start | bytes 32768 | tf_op jit(solution)/shard_map/all_to_all | solution.py:16
  19.3 0.0 copy-done.2
  19.3 11.7 %all-to-all-done.2 = s32[32,1,1,1]{3,2,1,0:T(1,128)S(1)} async-done(((s32[32,1,1,1]{3,2,1,0:T(1,128)}), s32[32,1,1,1]{3,2,1,0:T(1,128)S(1)}, u32[]{:S(2)}, u32[]{:S(2)}) %all-to-all-start.2) | async-done | bytes 160 | tf_op jit(solution)/shard_map/all_to_all | solution.py:16
  31.0 15.5 %all_to_all.30 = f32[32,2,4,128]{3,1,2,0:T(2,128)S(1)} all-to-all(f32[32,2,4,128]{3,1,2,0:T(2,128)S(1)} %broadcast_in_dim.13), channel_id=1, replica_groups=mesh['member'=16,'space'=32] {'space'}, dimensions={0} | all-to-all | bytes 262144 | tf_op jit(solution)/shard_map/all_to_all | solution.py:16
  46.5 0.0 copy-start
  46.5 4.8 %all-to-all-start = ((f32[128,2,4,128]{3,2,1,0:T(4,128)}), f32[128,2,4,128]{3,2,1,0:T(4,128)S(1)}, u32[]{:S(2)}, u32[]{:S(2)}) async-start(f32[128,2,4,128]{3,2,1,0:T(4,128)} %param.6), calls=%async_computation | async-start | bytes 1048576 | tf_op jit(solution)/shard_map/all_to_all | solution.py:460
  51.4 0.0 copy-done
  51.4 0.2 reshape.157
  51.6 0.1 reduce_sum.19
  51.8 0.7 reduce.8
  52.4 0.1 reshape_reshape.7
  52.5 0.1 copy.34
  52.6 0.1 copy.32
  52.6 0.7 copy.39
  53.4 15.6 %all-to-all-done = f32[128,2,4,128]{3,2,1,0:T(4,128)S(1)} async-done(((f32[128,2,4,128]{3,2,1,0:T(4,128)}), f32[128,2,4,128]{3,2,1,0:T(4,128)S(1)}, u32[]{:S(2)}, u32[]{:S(2)}) %all-to-all-start) | async-done | bytes 524320 | tf_op jit(solution)/shard_map/all_to_all | solution.py:460
  69.0 0.3 copy.29
  69.3 1.1 copy.30
  70.4 0.7 broadcast_in_dim.35.wanted
  71.1 42.7 %observed_pressure.1 = f32[32,4,128]{2,1,0:T(4,128)} custom-call(f32[4,32,8,128]{3,2,1,0:T(8,128)} %bitcast.47, f32[4,32,2,128]{3,2,1,0:T(2,128)} %bitcast.57, s32[16,8,128]{2,1,0:T(8,128)} %broadcast_in_dim.35.wanted), custom_call_target="tpu_custom_call" | custom-call | tf_op jit(solution)/shard_map/observed_pressure/pallas_call | solution.py:430
  113.8 0.0 copy-start.4
  113.8 9.0 %all-to-all-start.3 = ((f32[32,4,128]{2,1,0:T(4,128)}), f32[32,4,128]{2,1,0:T(4,128)S(1)}, u32[]{:S(2)}, u32[]{:S(2)}) async-start(f32[32,4,128]{2,1,0:T(4,128)} %observed_pressure.1), calls=%async_computation.3 | async-start | bytes 131072 | tf_op jit(solution)/shard_map/all_to_all | solution.py:468
  122.9 0.0 copy-done.4
  122.9 11.8 %all-to-all-done.3 = f32[32,4,128]{2,1,0:T(4,128)S(1)} async-done(((f32[32,4,128]{2,1,0:T(4,128)}), f32[32,4,128]{2,1,0:T(4,128)S(1)}, u32[]{:S(2)}, u32[]{:S(2)}) %all-to-all-start.3) | async-done | bytes 65568 | tf_op jit(solution)/shard_map/all_to_all | solution.py:468
  134.7 0.1 reduce_sum.18
  134.8 0.0 copy-start.1
  134.8 0.3 fusion.9
  135.0 0.0 copy-start.3
  135.1 0.6 copy-done.1
  135.6 0.1 copy-done.3
  135.7 0.1 multiply_add_fusion
  135.8 0.3 fusion.10
  136.0 0.7 pad_maximum_fusion
  136.7 28.7 %sum_everywhere.1 = f32[64,4,128]{2,1,0:T(4,128)} custom-call(f32[64,4,128]{2,1,0:T(4,128)} %bitcast.55), custom_call_target="tpu_custom_call" | custom-call | tf_op jit(solution)/shard_map/sum_everywhere/pallas_call | solution.py:120
  165.4 0.9 fusion.8
  166.3 0.1 copy.36
  166.4 11.7 %cholesky.16 = f32[128,128]{1,0:T(8,128)S(1)} custom-call(f32[128,128]{1,0:T(8,128)S(1)} %fusion.7), custom_call_target="Cholesky" | custom-call | tf_op jit(solution)/shard_map/jit(cholesky)/cholesky | solution.py:478
  178.2 0.6 compare_reduce_fusion
  178.8 0.7 fusion.2
  179.5 9.8 %custom-call.10 = f32[1,128,128]{1,2,0:T(8,128)S(1)} custom-call(f32[1,128,128]{2,1,0:T(8,128)S(1)} %fusion.2), custom_call_target="InvertDiagBlocksLowerTriangular" | custom-call | tf_op jit(solution)/shard_map/jit(_cho_solve)/triangular_solve | solution.py:481
  189.3 0.3 fusion.5
  189.6 0.2 fusion.3
  189.8 0.6 convolution_add_fusion
  190.4 1.0 reshape.162
  191.5 0.6 copy.42
  (10 shorter events, 0.1 us)
Async XLA Ops:
  1.9 17.4 %copy-start.2 = (f32[2,4,128]{2,1,0:T(4,128)S(1)}, f32[2,4,128]{2,1,0:T(4,128)}, u32[]{:S(2)}) copy-start(f32[2,4,128]{2,1,0:T(4,128)} %param.7) | copy-start | bytes 12292
  1.9 29.0 %all-to-all-start.2 = ((s32[32,1,1,1]{3,2,1,0:T(1,128)}), s32[32,1,1,1]{3,2,1,0:T(1,128)S(1)}, u32[]{:S(2)}, u32[]{:S(2)}) async-start(s32[32,1,1,1]{3,2,1,0:T(1,128)} %broadcast_in_dim.15), calls=%async_computation.2 | async-start | bytes 32768 | tf_op jit(solution)/shard_map/all_to_all | solution.py:16
  46.5 4.8 %copy-start = (f32[128,2,4,128]{3,2,1,0:T(4,128)S(1)}, f32[128,2,4,128]{3,2,1,0:T(4,128)}, u32[]{:S(2)}) copy-start(f32[128,2,4,128]{3,2,1,0:T(4,128)} %param.6) | copy-start | bytes 1572868
  46.5 22.5 %all-to-all-start = ((f32[128,2,4,128]{3,2,1,0:T(4,128)}), f32[128,2,4,128]{3,2,1,0:T(4,128)S(1)}, u32[]{:S(2)}, u32[]{:S(2)}) async-start(f32[128,2,4,128]{3,2,1,0:T(4,128)} %param.6), calls=%async_computation | async-start | bytes 1048576 | tf_op jit(solution)/shard_map/all_to_all | solution.py:460
  113.8 9.0 %copy-start.4 = (f32[1,1,128]{2,1,0:T(1,128)S(1)}, f32[1,1,128]{2,1,0:T(1,128)}, u32[]{:S(2)}) copy-start(f32[1,1,128]{2,1,0:T(1,128)} %param.11) | copy-start | bytes 1540
  113.8 20.9 %all-to-all-start.3 = ((f32[32,4,128]{2,1,0:T(4,128)}), f32[32,4,128]{2,1,0:T(4,128)S(1)}, u32[]{:S(2)}, u32[]{:S(2)}) async-start(f32[32,4,128]{2,1,0:T(4,128)} %observed_pressure.1), calls=%async_computation.3 | async-start | bytes 131072 | tf_op jit(solution)/shard_map/all_to_all | solution.py:468
  134.8 0.8 copy-start.1
  135.0 0.7 copy-start.3

commit v3 on v2

--- a/solution.py
+++ b/solution.py
@@ -9,22 +9,6 @@
 WIDE = 8
 
 ITERS = 4
-
-
-def from_everyone(x, axis):
-    devices = lax.axis_size(axis)
-    return lax.all_to_all(jnp.broadcast_to(x[None], (devices, *x.shape)), axis, 0, 0, tiled=True)
-
-
-def joined_along(pieces, dim):
-    shape = list(pieces.shape[1:])
-    shape[dim] *= pieces.shape[0]
-    return jnp.moveaxis(pieces, 0, dim).reshape(shape)
-
-
-def collect(x, axis, dim):
-    pieces = from_everyone(x, axis)
-    return joined_along(pieces, dim)
 
 
 def place():
@@ -144,14 +128,21 @@
 
 HALF = 32
 TEAM = 16
+SPACE = 32
 COND, SOURCE = ITERS - 1, ITERS
 
 
 def conjugate_kernel(
-    field,
+    ensemble,
     source,
     wanted,
+    predicted,
+    held_rows,
+    held_source,
+    held_wanted,
     picked,
+    returned,
+    side,
     cond,
     face_x,
     face_y,
@@ -172,8 +163,12 @@
     edge_recv,
     tile_send,
     tile_recv,
+    swap_send,
+    swap_recv,
+    own_sems,
 ):
     member = lax.axis_index("member")
+    space = lax.axis_index("space")
     plane = (8, 128)
     sublane = lax.broadcasted_iota(jnp.int32, plane, 0)
     lane = lax.broadcasted_iota(jnp.int32, plane, 1)
@@ -185,9 +180,9 @@
 
     def edge_copy(kind, upward):
         if kind == COND:
-            origin, target = field.at[3 * upward], cond_edge.at[1 - upward]
+            origin, target = cond.at[3 * upward, pl.ds(1, HALF)], cond_edge.at[1 - upward]
         elif kind == SOURCE:
-            origin, target = source.at[3 * upward], source_edge.at[1 - upward]
+            origin, target = side.at[upward], source_edge.at[1 - upward]
         else:
             origin, target = searched.at[3 * upward, pl.ds(1, HALF)], edges.at[kind, 1 - upward]
         return pltpu.make_async_remote_copy(
@@ -230,11 +225,42 @@
         return pltpu.make_async_remote_copy(
             src_ref=tiles.at[turn, member],
             dst_ref=tiles.at[turn, member],
-            send_sem=tile_send.at[turn, step - 1],
-            recv_sem=tile_recv.at[turn, step - 1],
+            send_sem=tile_send.at[turn],
+            recv_sem=tile_recv.at[turn],
             device_id=team_peer(step),
             device_id_type=pl.DeviceIdType.MESH,
         )
+
+    def wait_bytes(ref, sem):
+        pltpu.make_async_copy(ref, ref, sem).wait()
+
+    def space_peer(step):
+        other = lax.rem(space + step, SPACE)
+        return other, {"space": other}
+
+    def halves(index):
+        return lax.rem(index, HALF // 2), lax.div(index, HALF // 2)
+
+    def piece_refs(other):
+        block, half = halves(space)
+        rows = pl.ds(pl.multiple_of(half * 32, 32), 32)
+        return (
+            (ensemble.at[pl.ds(pl.multiple_of(other * 32, 32), 32)], held_rows.at[block, rows]),
+            (source, held_source.at[block, pl.ds(pl.multiple_of(half * 8, 8), 8)]),
+            (wanted, held_wanted.at[space]),
+        )
+
+    def swap(step):
+        other, device = space_peer(step)
+        for kind, (origin, target) in enumerate(piece_refs(other)):
+            pltpu.make_async_remote_copy(
+                src_ref=origin,
+                dst_ref=target,
+                send_sem=swap_send.at[kind],
+                recv_sem=swap_recv.at[kind],
+                device_id=device,
+                device_id_type=pl.DeviceIdType.MESH,
+            ).start()
 
     def send_sums(turn, norm, product):
         norm = norm + pltpu.roll(norm, 64, 1)
@@ -244,47 +270,57 @@
             tile_copy(turn, step).start()
 
     def sums_here(turn):
-        for step in range(1, TEAM):
-            tile_copy(turn, step).wait_recv()
+        wait_bytes(tiles.at[turn, pl.ds(0, TEAM - 1)], tile_recv.at[turn])
         both = jnp.sum(tiles[turn], axis=0)
         both = both + pltpu.roll(both, 4, 0)
         norm = jnp.sum(jnp.where(lane < 64, both, 0.0), axis=1, keepdims=True)
         product = jnp.sum(jnp.where(lane < 64, 0.0, both), axis=1, keepdims=True)
         return jnp.broadcast_to(norm, plane), jnp.broadcast_to(product, plane)
 
-    def over_rows(body, start, width=2):
+    def over_rows(body, start):
         def several(block, carry):
-            for k in range(width):
-                carry = body(block * width + k, carry)
+            for k in range(2):
+                carry = body(block, k, carry)
             return carry
 
-        return lax.fori_loop(0, HALF // width, several, start)
+        return lax.fori_loop(0, HALF // 2, several, start)
 
     barrier = pltpu.get_barrier_semaphore()
+    for step in range(1, SPACE):
+        pl.semaphore_signal(barrier, inc=1, device_id=space_peer(step)[1], device_id_type=pl.DeviceIdType.MESH)
     for step in range(1, TEAM):
         pl.semaphore_signal(barrier, inc=1, device_id=team_peer(step), device_id_type=pl.DeviceIdType.MESH)
-    pl.semaphore_wait(barrier, TEAM - 1)
-    send_edges(COND)
-    send_edges(SOURCE)
+    own = [
+        pltpu.make_async_copy(origin, target, own_sems.at[kind])
+        for kind, (origin, target) in enumerate(piece_refs(space))
+    ]
+    for copy in own:
+        copy.start()
+    pl.semaphore_wait(barrier, TEAM + SPACE - 2)
+    for step in range(1, SPACE):
+        swap(step)
 
     @pl.when(member == 0)
     def _():
-        cond_edge[0] = field[0]
         source_edge[0] = jnp.zeros(source_edge.shape[1:], jnp.float32)
         for kind in range(ITERS - 1):
             edges[kind, 0] = jnp.zeros(edges.shape[2:], jnp.float32)
 
     @pl.when(member == TEAM - 1)
     def _():
-        cond_edge[1] = field[3]
         source_edge[1] = jnp.zeros(source_edge.shape[1:], jnp.float32)
         for kind in range(ITERS - 1):
             edges[kind, 1] = jnp.zeros(edges.shape[2:], jnp.float32)
 
-    def spread_source(rows):
-        lower, upper = rows[..., 0:1, :], rows[..., 1:2, :]
-        shape = (*rows.shape[:-2], *plane)
-        return jnp.where(low_half, jnp.broadcast_to(lower, shape), jnp.broadcast_to(upper, shape))
+    for copy in own:
+        copy.wait()
+    others = SPACE - 1
+    wait_bytes(ensemble.at[pl.ds(0, others * 32)], swap_recv.at[0])
+    wait_bytes(ensemble.at[pl.ds(0, others * 8)], swap_recv.at[1])
+    wait_bytes(held_wanted.at[pl.ds(0, others)], swap_recv.at[2])
+
+    def two_rows(lower, upper):
+        return jnp.where(low_half, jnp.broadcast_to(lower, plane), jnp.broadcast_to(upper, plane))
 
     def close_ends(padded, outside):
         for y in range(4):
@@ -294,16 +330,35 @@
             padded[y, 0] = jnp.where(low_half, below, pltpu.roll(last, 4, 0))
             padded[y, HALF + 1] = jnp.where(low_half, pltpu.roll(first, 4, 0), above)
 
-    def begin(row, carry):
-        cond[:, row + 1] = jnp.exp(field[:, row])
-        searched[:, row + 1] = spread_source(source[:, row])
+    def begin(block, carry):
+        rows = held_source[block]
+        for k in range(2):
+            for y in range(4):
+                at = 4 * k + y
+                held = held_rows[block, pl.ds(at, 8, stride=8), :]
+                cond[y, 2 * block + k + 1] = jnp.exp(held)
+                searched[y, 2 * block + k + 1] = two_rows(rows[at : at + 1], rows[8 + at : 9 + at])
+        for upward in range(2):
+            at = 3 * upward
+            side[upward, block] = jnp.concatenate([rows[at + k : at + k + 1] for k in (0, 8, 4, 12)])
         return carry
 
-    over_rows(begin, 0)
+    lax.fori_loop(0, HALF // 2, begin, 0)
+    send_edges(COND)
+    send_edges(SOURCE)
     close_ends(cond, None)
     close_ends(searched, jnp.zeros(plane, jnp.float32))
 
-    def inner_faces(row, carry):
+    @pl.when(member == 0)
+    def _():
+        cond_edge[0] = cond[0, pl.ds(1, HALF)]
+
+    @pl.when(member == TEAM - 1)
+    def _():
+        cond_edge[1] = cond[3, pl.ds(1, HALF)]
+
+    def inner_faces(block, k, carry):
+        row = 2 * block + k
         here = cond[:, row + 1]
         face_x[:, row + 1] = harmonic(here, cond[:, row + 2])
         above = jnp.where(lane_4 == 127, here, pltpu.roll(here, 127, 2))
@@ -318,18 +373,20 @@
         face_x[y, 0] = harmonic(cond[y, 0], cond[y, 1])
     edges_here(COND)
 
-    def outer_faces(row, carry):
-        face_y[0, row] = harmonic(jnp.exp(cond_edge[0, row]), cond[0, row + 1])
-        face_y[4, row] = harmonic(cond[3, row + 1], jnp.exp(cond_edge[1, row]))
+    def outer_faces(block, k, carry):
+        row = 2 * block + k
+        face_y[0, row] = harmonic(cond_edge[0, row], cond[0, row + 1])
+        face_y[4, row] = harmonic(cond[3, row + 1], cond_edge[1, row])
         return carry
 
     over_rows(outer_faces, 0)
 
     def operate(lower_edge, upper_edge):
-        def body(row, carry):
+        def body(block, k, carry):
+            row = 2 * block + k
             here = searched[:, row + 1]
-            before = jnp.concatenate([lower_edge(row)[None], here[:3]])
-            after = jnp.concatenate([here[1:], upper_edge(row)[None]])
+            before = jnp.concatenate([lower_edge(block, k)[None], here[:3]])
+            after = jnp.concatenate([here[1:], upper_edge(block, k)[None]])
             result = face_x[:, row + 1] * (here - searched[:, row + 2])
             result = result + face_x[:, row] * (here - searched[:, row])
             result = result + face_y[1:5, row] * (here - after)
@@ -344,9 +401,18 @@
 
     zeros = jnp.zeros(plane, jnp.float32)
     edges_here(SOURCE)
-    operate(lambda row: spread_source(source_edge[0, row]), lambda row: spread_source(source_edge[1, row]))
-
-    def first_sums(row, carry):
+
+    def source_side(upward):
+        def rows(block, k):
+            four = source_edge[upward, block]
+            return two_rows(four[2 * k : 2 * k + 1], four[2 * k + 1 : 2 * k + 2])
+
+        return rows
+
+    operate(source_side(0), source_side(1))
+
+    def first_sums(block, k, carry):
+        row = 2 * block + k
         norm, product = carry
         image_here = image[:, row]
         residual_here = searched[:, row + 1]
@@ -366,7 +432,7 @@
             send_edges(turn)
             close_ends(searched, zeros)
             edges_here(turn)
-            operate(lambda row: edges[turn, 0, row], lambda row: edges[turn, 1, row])
+            operate(lambda block, k: edges[turn, 0, 2 * block + k], lambda block, k: edges[turn, 1, 2 * block + k])
         norm_now, product_now = sums_here(turn)
         if turn == 0:
             step_size = norm_now / product_now
@@ -375,7 +441,8 @@
             step_size = norm_now / (product_now - ratio * norm_now / step_before)
         norm_before, step_before = norm_now, step_size
 
-        def update(row, carry):
+        def update(block, k, carry):
+            row = 2 * block + k
             norm, product = carry
             residual_here, image_here = residual[:, row], searched[:, row + 1]
             direction_here, along_here, beyond_here = residual_here, image_here, image[:, row]
@@ -397,7 +464,8 @@
                 residual_here * image_here, axis=0
             )
 
-        def finish(row, carry):
+        def finish(block, k, carry):
+            row = 2 * block + k
             answer[:, row] = answer[:, row] + step_size * (residual[:, row] + ratio * direction[:, row])
             return carry
 
@@ -408,64 +476,82 @@
             norm, product = over_rows(update, (zeros, zeros))
 
     for block in range(HALF // 2):
-        chosen = wanted[block]
+        chosen = two_rows(held_wanted[block], held_wanted[HALF // 2 + block])
         value = zeros
         for choice in range(8):
             value = value + jnp.where(chosen == choice, answer[choice % 4, 2 * block + choice // 4], 0.0)
         picked[block] = value[:4]
         picked[HALF // 2 + block] = value[4:]
 
+    returned[space] = picked[space]
+    for step in range(1, SPACE):
+        other, device = space_peer(step)
+        pltpu.make_async_remote_copy(
+            src_ref=picked.at[other],
+            dst_ref=returned.at[space],
+            send_sem=swap_send.at[3],
+            recv_sem=swap_recv.at[3],
+            device_id=device,
+            device_id_type=pl.DeviceIdType.MESH,
+        ).start()
+    wait_bytes(returned.at[pl.ds(0, others)], swap_recv.at[3])
+    predicted[...] = returned[...]
+
     edges_sent(COND)
     edges_sent(SOURCE)
     for turn in range(ITERS):
-        for step in range(1, TEAM):
-            tile_copy(turn, step).wait_send()
-
-
-def observed_pressure(field, source, wanted):
-    held = field.shape
-    padded = (held[0], held[1] + 2, *held[2:])
-    edge = held[1:]
+        wait_bytes(tiles.at[turn, pl.ds(0, TEAM - 1)], tile_send.at[turn])
+    wait_bytes(ensemble.at[pl.ds(0, others * 32)], swap_send.at[0])
+    wait_bytes(ensemble.at[pl.ds(0, others * 8)], swap_send.at[1])
+    wait_bytes(held_wanted.at[pl.ds(0, others)], swap_send.at[2])
+    wait_bytes(returned.at[pl.ds(0, others)], swap_send.at[3])
+
+
+def predict(ensemble, source, wanted):
+    held = (4, HALF, 8, 128)
+    padded = (4, HALF + 2, 8, 128)
     vmem = lambda *shape: pltpu.VMEM(shape, jnp.float32)
     return pl.pallas_call(
         conjugate_kernel,
-        out_shape=jax.ShapeDtypeStruct((HALF, 4, 128), jnp.float32),
-        in_specs=[pl.BlockSpec(memory_space=pltpu.VMEM)] * 3,
+        out_shape=jax.ShapeDtypeStruct((SPACE, 4, 128), jnp.float32),
+        in_specs=[pl.BlockSpec(memory_space=pl.ANY), *[pl.BlockSpec(memory_space=pltpu.VMEM)] * 2],
         out_specs=pl.BlockSpec(memory_space=pltpu.VMEM),
         scratch_shapes=[
+            vmem(HALF // 2, 64, 128),
+            vmem(HALF // 2, 16, 128),
+            pltpu.VMEM((SPACE, 1, 128), jnp.int32),
+            vmem(SPACE, 4, 128),
+            vmem(SPACE, 4, 128),
+            vmem(2, HALF // 2, 4, 128),
             vmem(*padded),
-            vmem(held[0], held[1] + 1, *held[2:]),
-            vmem(held[0] + 1, *held[1:]),
+            vmem(4, HALF + 1, 8, 128),
+            vmem(5, HALF, 8, 128),
             vmem(*held),
             vmem(*held),
             vmem(*padded),
             *[vmem(*held)] * 6,
-            vmem(2, *edge),
-            vmem(2, *source.shape[1:]),
-            vmem(ITERS - 1, 2, *edge),
-            vmem(ITERS, TEAM, *held[2:]),
+            vmem(2, HALF, 8, 128),
+            vmem(2, HALF // 2, 4, 128),
+            vmem(ITERS - 1, 2, HALF, 8, 128),
+            vmem(ITERS, TEAM, 8, 128),
             pltpu.SemaphoreType.DMA((ITERS + 1, 2)),
             pltpu.SemaphoreType.DMA((ITERS + 1, 2)),
-            pltpu.SemaphoreType.DMA((ITERS, TEAM - 1)),
-            pltpu.SemaphoreType.DMA((ITERS, TEAM - 1)),
+            pltpu.SemaphoreType.DMA((ITERS,)),
+            pltpu.SemaphoreType.DMA((ITERS,)),
+            pltpu.SemaphoreType.DMA((4,)),
+            pltpu.SemaphoreType.DMA((4,)),
+            pltpu.SemaphoreType.DMA((3,)),
         ],
         compiler_params=pltpu.CompilerParams(collective_id=2, has_side_effects=True),
-        name="observed_pressure",
-    )(field, source, wanted)
+        name="predict",
+    )(ensemble, source, wanted)
 
 
 def local(ensemble, source, obs_rows, obs_values, obs_noise, obs_var):
     total_members = ensemble.shape[0]
-    block_x, block_y, layers = source.shape
-    held_fields = lax.all_to_all(ensemble, "space", split_axis=0, concat_axis=1, tiled=True)
-    held_count = held_fields.shape[0]
-    field = held_fields.reshape(held_count, 2, HALF, block_y, layers).transpose(3, 2, 1, 0, 4)
-    field = field.reshape(block_y, HALF, 2 * held_count, layers)
-    forcing = collect(source, "space", 0).reshape(2, HALF, block_y, layers).transpose(2, 1, 0, 3)
-    gathered_rows = collect(obs_rows, "space", 0).reshape(2, -1).T
-    wanted = jnp.broadcast_to(gathered_rows[:, :, None, None], (HALF // 2, 2, held_count, layers))
-    picked = observed_pressure(field, forcing, wanted.reshape(HALF // 2, 2 * held_count, layers))
-    returned = lax.all_to_all(picked, "space", split_axis=0, concat_axis=0, tiled=True)
+    layers = source.shape[-1]
+    wanted = jnp.broadcast_to(obs_rows.reshape(1, 1), (1, layers))
+    returned = predict(ensemble.reshape(-1, layers), source.reshape(-1, layers), wanted)
     predicted = returned.reshape(total_members, 1, 1, -1)
     flat_pred = returned.reshape(total_members, -1)
     inv_sigma = 1.0 / jnp.sqrt(obs_var.reshape(-1))

time: 193 us -> 146 us (0.76)
  Pallas kernels: 71.3 us -> 112 us
  waiting for transfers between devices: 39.1 us -> 0 us
  starting transfers between devices: 31.2 us -> 0 us
  blocking collectives: 15.5 us -> 0 us
  local copies, waits for them, and re-layouts: 7.25 us -> 4.83 us
    pallas_call x1, Pallas kernels: 42.7 us -> 83.8 us  [predict(): pl.pallas_call(conjugate_kernel, out_shape=jax.ShapeDtypeStruct((SPACE, 4...]
    all_to_all x3 -> x0, waiting for transfers between devices: 39.1 us -> none  [the longest x1 15.6 us: local(): lax.all_to_all(ensemble, 'space', split_axis=0, concat_axis=1, tiled=True)]
    all_to_all x3 -> x0, starting transfers between devices: 31.2 us -> none  [the longest x1 17.4 us: from_everyone(): lax.all_to_all(jnp.broadcast_to(x[None], (devices, *x.shape)), axis, 0, 0...]
    all_to_all x1 -> x0, blocking collectives: 15.5 us -> none  [from_everyone(): lax.all_to_all(jnp.broadcast_to(x[None], (devices, *x.shape)), axis, 0, 0...]
  transfers between devices with their start and end apart: 3 -> 0, of which waited for: 3 -> 0; matrix products, arithmetic and copies ran while one was open for 1% -> 0% of each run, Pallas kernels for 0% -> 0%
where the time goes in v3:
time: 146 us
  Pallas kernels  112 us (77%)
  other arithmetic  25.8 us (18%)
  local copies, waits for them, and re-layouts  4.83 us (3%)
  matrix products  1.65 us (1%)
    pallas_call x1, Pallas kernels, predict(): pl.pallas_call(conjugate_kernel, out_shape=jax.ShapeDtypeStruct((SPACE, 4...  83.8 us
    pallas_call x1, Pallas kernels, sum_everywhere(): pl.pallas_call(sum_kernel, out_shape=jax.ShapeDtypeStruct(part.shape, jnp...  28.5 us
    another operation x3, other arithmetic, local(): jnp.linalg.cholesky(gram_sum + (total_members - 1.0) * jnp.eye(total_memb...  12.4 us
    another operation x2, other arithmetic, local(): weights = jax.scipy.linalg.cho_solve((factor, True), cross_sum)  10.5 us

profile of v3, /device:TPU:1, one launch (start us, length us, event | category | flops | bytes accessed | tf_op | source)
XLA Modules:
  0.0 146.0 jit_solution(17067109973128265999)
XLA Ops:
  1.3 0.5 broadcast_in_dim.6.wanted
  1.8 0.0 copy-start.4
  1.8 0.7 copy-done.4
  2.4 1.2 reduce_sum.19
  3.7 83.8 %predict.1 = f32[32,4,128]{2,1,0:T(4,128)} custom-call(f32[1024,128]{1,0:T(8,128)} %bitcast.35, f32[8,128]{1,0:T(8,128)} %bitcast.46, s32[1,128]{1,0:T(1,128)} %broadcast_in_dim.6.wanted), custom_call_target="tpu_custom_call" | custom-call | tf_op jit(solution)/shard_map/predict/pallas_call | solution.py:514
  87.5 0.0 copy-start.1
  87.5 1.0 reduce_sum.18
  88.5 0.0 copy-done.1
  88.5 0.0 copy-start.2
  88.5 0.0 copy-start.3
  88.5 0.8 copy-done.2
  89.3 0.0 copy-done.3
  89.3 0.1 multiply_add_fusion
  89.4 0.3 fusion.10
  89.7 0.3 fusion.9
  89.9 0.7 pad_maximum_fusion
  90.6 28.5 %sum_everywhere.1 = f32[64,4,128]{2,1,0:T(4,128)} custom-call(f32[64,4,128]{2,1,0:T(4,128)} %bitcast.42), custom_call_target="tpu_custom_call" | custom-call | tf_op jit(solution)/shard_map/sum_everywhere/pallas_call | solution.py:104
  119.1 0.9 fusion.8
  119.9 0.0 copy-start
  120.0 0.1 copy.9
  120.1 11.7 %cholesky.16 = f32[128,128]{1,0:T(8,128)S(1)} custom-call(f32[128,128]{1,0:T(8,128)S(1)} %fusion.7), custom_call_target="Cholesky" | custom-call | tf_op jit(solution)/shard_map/jit(cholesky)/cholesky | solution.py:564
  131.9 0.6 compare_reduce_fusion
  132.5 0.7 fusion.2
  133.2 9.8 %custom-call.10 = f32[1,128,128]{1,2,0:T(8,128)S(1)} custom-call(f32[1,128,128]{2,1,0:T(8,128)S(1)} %fusion.2), custom_call_target="InvertDiagBlocksLowerTriangular" | custom-call | tf_op jit(solution)/shard_map/jit(_cho_solve)/triangular_solve | solution.py:567
  143.0 0.3 fusion.5
  143.3 0.2 fusion.3
  143.5 0.0 copy-done
  143.5 0.2 reshape.153
  143.7 0.6 convolution_add_fusion
  144.3 1.0 reshape.158
  145.4 0.6 copy.13
  (7 shorter events, 0.1 us)
Async XLA Ops:
  1.8 0.7 copy-start.4
  87.5 1.0 copy-start.1
  88.5 0.8 copy-start.2
  88.5 0.8 copy-start.3
  119.9 23.5 %copy-start = (f32[128,2,4,128]{3,2,1,0:T(4,128)S(1)}, f32[128,2,4,128]{3,2,1,0:T(4,128)}, u32[]{:S(2)}) copy-start(f32[128,2,4,128]{3,2,1,0:T(4,128)} %param.6) | copy-start | bytes 1572868

commit v4 on v3

--- a/solution.py
+++ b/solution.py
@@ -1,3 +1,5 @@
+import functools
+
 import jax
 import jax.numpy as jnp
 from jax import lax
@@ -26,7 +28,7 @@
     return {"member": member, "space": space}
 
 
-def sum_kernel(part, total, got_row, sum_row, got_y, sum_y, got_z, all_y, all_row, send_sems, recv_sems):
+def sum_peers():
     x, y, z, core = place()
     row = x * CORES + core
 
@@ -42,11 +44,11 @@
         other = lax.rem(z + step, WIDE)
         return other, device_at(x, y, other, core)
 
-    barrier = pltpu.get_barrier_semaphore()
-    for peer in (row_peer, y_peer, z_peer):
-        for step in range(1, WIDE):
-            pl.semaphore_signal(barrier, inc=1, device_id=peer(step)[1], device_id_type=pl.DeviceIdType.MESH)
-    pl.semaphore_wait(barrier, 3 * (WIDE - 1))
+    return (row, y, z), (row_peer, y_peer, z_peer)
+
+
+def sum_everywhere(part, total, got_row, sum_row, got_y, sum_y, got_z, all_y, all_row, send_sems, recv_sems):
+    (row, y, z), (row_peer, y_peer, z_peer) = sum_peers()
 
     def exchange(phase, peer, source, target):
         copies = []
@@ -94,32 +96,11 @@
     sent += copies
     all_row[row] = all_y[...]
     arrived(copies)
-    total[...] = all_row[...].reshape(total.shape)
+    for i in range(WIDE):
+        for j in range(0, WIDE, 2):
+            total[pl.ds(4 * (WIDE * i + j), 8)] = jnp.concatenate([all_row[i, j], all_row[i, j + 1]])
     for copy in sent:
         copy.wait_send()
-
-
-def sum_everywhere(part):
-    dims = part.shape[1:]
-    return pl.pallas_call(
-        sum_kernel,
-        out_shape=jax.ShapeDtypeStruct(part.shape, jnp.float32),
-        in_specs=[pl.BlockSpec(memory_space=pltpu.VMEM)],
-        out_specs=pl.BlockSpec(memory_space=pltpu.VMEM),
-        scratch_shapes=[
-            pltpu.VMEM((WIDE - 1, WIDE, *dims), jnp.float32),
-            pltpu.VMEM((WIDE, *dims), jnp.float32),
-            pltpu.VMEM((WIDE - 1, *dims), jnp.float32),
-            pltpu.VMEM(dims, jnp.float32),
-            pltpu.VMEM((WIDE, *dims), jnp.float32),
-            pltpu.VMEM((WIDE, *dims), jnp.float32),
-            pltpu.VMEM((WIDE, WIDE, *dims), jnp.float32),
-            pltpu.SemaphoreType.DMA((5, WIDE - 1)),
-            pltpu.SemaphoreType.DMA((5, WIDE - 1)),
-        ],
-        compiler_params=pltpu.CompilerParams(collective_id=1, has_side_effects=True),
-        name="sum_everywhere",
-    )(part)
 
 
 def harmonic(first_cond, second_cond):
@@ -136,7 +117,11 @@
     ensemble,
     source,
     wanted,
+    obs_values,
+    obs_noise,
+    obs_var,
     predicted,
+    total,
     held_rows,
     held_source,
     held_wanted,
@@ -166,6 +151,8 @@
     swap_send,
     swap_recv,
     own_sems,
+    part,
+    *sum_refs,
 ):
     member = lax.axis_index("member")
     space = lax.axis_index("space")
@@ -290,13 +277,16 @@
         pl.semaphore_signal(barrier, inc=1, device_id=space_peer(step)[1], device_id_type=pl.DeviceIdType.MESH)
     for step in range(1, TEAM):
         pl.semaphore_signal(barrier, inc=1, device_id=team_peer(step), device_id_type=pl.DeviceIdType.MESH)
+    for peer in sum_peers()[1]:
+        for step in range(1, WIDE):
+            pl.semaphore_signal(barrier, inc=1, device_id=peer(step)[1], device_id_type=pl.DeviceIdType.MESH)
     own = [
         pltpu.make_async_copy(origin, target, own_sems.at[kind])
         for kind, (origin, target) in enumerate(piece_refs(space))
     ]
     for copy in own:
         copy.start()
-    pl.semaphore_wait(barrier, TEAM + SPACE - 2)
+    pl.semaphore_wait(barrier, TEAM - 1 + SPACE - 1 + 3 * (WIDE - 1))
     for step in range(1, SPACE):
         swap(step)
 
@@ -495,7 +485,20 @@
             device_id_type=pl.DeviceIdType.MESH,
         ).start()
     wait_bytes(returned.at[pl.ds(0, others)], swap_recv.at[3])
-    predicted[...] = returned[...]
+    for i in range(SPACE // 2):
+        predicted[pl.ds(8 * i, 8)] = jnp.concatenate([returned[2 * i], returned[2 * i + 1]])
+
+    values = predicted[...]
+    inverse_sigma = 1.0 / jnp.sqrt(obs_var[...])
+    spread = (values - jnp.mean(values, axis=0, keepdims=True)) * inverse_sigma
+    misfit = (obs_values[...] - values) * inverse_sigma + obs_noise[...]
+    for i, other in enumerate((spread, misfit)):
+        product = lax.dot_general(
+            spread, other, (((1,), (1,)), ((), ())), precision=lax.Precision.HIGHEST, preferred_element_type=jnp.float32
+        )
+        for j in range(HALF):
+            part[HALF * i + j] = product[4 * j : 4 * j + 4]
+    sum_everywhere(part, total, *sum_refs)
 
     edges_sent(COND)
     edges_sent(SOURCE)
@@ -507,15 +510,15 @@
     wait_bytes(returned.at[pl.ds(0, others)], swap_send.at[3])
 
 
-def predict(ensemble, source, wanted):
+def predict(ensemble, source, wanted, obs_values, obs_noise, obs_var):
     held = (4, HALF, 8, 128)
     padded = (4, HALF + 2, 8, 128)
     vmem = lambda *shape: pltpu.VMEM(shape, jnp.float32)
     return pl.pallas_call(
         conjugate_kernel,
-        out_shape=jax.ShapeDtypeStruct((SPACE, 4, 128), jnp.float32),
-        in_specs=[pl.BlockSpec(memory_space=pl.ANY), *[pl.BlockSpec(memory_space=pltpu.VMEM)] * 2],
-        out_specs=pl.BlockSpec(memory_space=pltpu.VMEM),
+        out_shape=[jax.ShapeDtypeStruct((rows, 128), jnp.float32) for rows in (128, 256)],
+        in_specs=[pl.BlockSpec(memory_space=pl.ANY), *[pl.BlockSpec(memory_space=pltpu.VMEM)] * 5],
+        out_specs=[pl.BlockSpec(memory_space=pltpu.VMEM)] * 2,
         scratch_shapes=[
             vmem(HALF // 2, 64, 128),
             vmem(HALF // 2, 16, 128),
@@ -541,34 +544,113 @@
             pltpu.SemaphoreType.DMA((4,)),
             pltpu.SemaphoreType.DMA((4,)),
             pltpu.SemaphoreType.DMA((3,)),
+            vmem(64, 4, 128),
+            vmem(WIDE - 1, WIDE, 4, 128),
+            vmem(WIDE, 4, 128),
+            vmem(WIDE - 1, 4, 128),
+            vmem(4, 128),
+            vmem(WIDE, 4, 128),
+            vmem(WIDE, 4, 128),
+            vmem(WIDE, WIDE, 4, 128),
+            pltpu.SemaphoreType.DMA((5, WIDE - 1)),
+            pltpu.SemaphoreType.DMA((5, WIDE - 1)),
         ],
         compiler_params=pltpu.CompilerParams(collective_id=2, has_side_effects=True),
         name="predict",
-    )(ensemble, source, wanted)
+    )(ensemble, source, wanted, obs_values, obs_noise, obs_var)
+
+
+PANEL = 8
+
+
+def solve_kernel(total, ensemble, updated, gram, cross, scaled, weights):
+    plane = (PANEL, 128)
+    count = gram.shape[0]
+    sublane = lax.broadcasted_iota(jnp.int32, plane, 0)
+    lane = lax.broadcasted_iota(jnp.int32, plane, 1)
+    whole = functools.partial(lax.dot_general, precision=lax.Precision.HIGHEST, preferred_element_type=jnp.float32)
+
+    def spread(row):
+        return jnp.broadcast_to(row, plane)
+
+    for low in range(0, count, PANEL):
+        gram[low : low + PANEL] = total[low : low + PANEL] + jnp.where(lane == sublane + low, count - 1.0, 0.0)
+    cross[...] = total[count:]
+
+    for low in range(0, count, PANEL):
+        rows_g, rows_c = gram[low : low + PANEL], cross[low : low + PANEL]
+        columns = [spread(rows_g[:, low + j : low + j + 1]) for j in range(PANEL)]
+        pivots = {(i, j): spread(columns[j][i : i + 1]) for j in range(PANEL) for i in range(j + 1)}
+        inverse, factor = [], {}
+        for k in range(PANEL):
+            inverse.append(1.0 / pivots[k, k])
+            for i in range(k + 1, PANEL):
+                factor[i, k] = pivots[k, i] * inverse[k]
+                for j in range(i, PANEL):
+                    pivots[i, j] = pivots[i, j] - factor[i, k] * pivots[k, j]
+        solved = []
+        for rows in (rows_g, rows_c):
+            lines = [spread(rows[i : i + 1]) for i in range(PANEL)]
+            for k in range(PANEL):
+                for i in range(k + 1, PANEL):
+                    lines[i] = lines[i] - factor[i, k] * lines[k]
+            lines = [line * inverse[i] for i, line in enumerate(lines)]
+            for k in reversed(range(PANEL)):
+                for i in range(k):
+                    lines[i] = lines[i] - factor[k, i] * lines[k]
+            joined = lines[0]
+            for i in range(1, PANEL):
+                joined = jnp.where(sublane == i, lines[i], joined)
+            solved.append(joined)
+        scaled[low : low + PANEL] = solved[0]
+        weights[low : low + PANEL] = solved[1]
+        after = low + PANEL
+        if after < count:
+            taken = rows_g.T
+            gram[after:] = gram[after:] - whole(taken, solved[0], (((1,), (0,)), ((), ())))[after:]
+            cross[after:] = cross[after:] - whole(taken, solved[1], (((1,), (0,)), ((), ())))[after:]
+
+    for low in range(count - 2 * PANEL, -1, -PANEL):
+        known = low + PANEL
+        left = jnp.where(lane >= known, scaled[low : low + PANEL], 0.0)
+        weights[low : low + PANEL] = weights[low : low + PANEL] - whole(left, weights[...], (((1,), (0,)), ((), ())))
+
+    turned = weights[...].T
+    for row in range(PANEL):
+        picks = [pl.ds(row + 8 * PANEL * i, PANEL, stride=8) for i in range(count // PANEL)]
+        fields = [ensemble[pick, :] for pick in picks]
+        mean = jnp.sum(sum(fields), axis=0, keepdims=True) * (1.0 / count)
+        change = whole(turned, jnp.concatenate([field - mean for field in fields]), (((1,), (0,)), ((), ())))
+        for i, pick in enumerate(picks):
+            updated[pick, :] = fields[i] + change[PANEL * i : PANEL * (i + 1)]
+
+
+def solve_and_update(total, ensemble):
+    square = pltpu.VMEM((total.shape[1], total.shape[1]), jnp.float32)
+    return pl.pallas_call(
+        solve_kernel,
+        out_shape=jax.ShapeDtypeStruct(ensemble.shape, jnp.float32),
+        in_specs=[pl.BlockSpec(memory_space=pltpu.VMEM)] * 2,
+        out_specs=pl.BlockSpec(memory_space=pltpu.VMEM),
+        scratch_shapes=[square] * 4,
+        name="solve_and_update",
+    )(total, ensemble)
 
 
 def local(ensemble, source, obs_rows, obs_values, obs_noise, obs_var):
-    total_members = ensemble.shape[0]
     layers = source.shape[-1]
+    fields = ensemble.reshape(-1, layers)
     wanted = jnp.broadcast_to(obs_rows.reshape(1, 1), (1, layers))
-    returned = predict(ensemble.reshape(-1, layers), source.reshape(-1, layers), wanted)
-    predicted = returned.reshape(total_members, 1, 1, -1)
-    flat_pred = returned.reshape(total_members, -1)
-    inv_sigma = 1.0 / jnp.sqrt(obs_var.reshape(-1))
-    spread = (flat_pred - jnp.mean(flat_pred, axis=0)) * inv_sigma
-    misfit = (obs_values.reshape(-1) - flat_pred) * inv_sigma + obs_noise.reshape(total_members, -1)
-    gram_part = jnp.dot(spread, spread.T, precision=lax.Precision.HIGHEST)
-    cross_part = jnp.dot(spread, misfit.T, precision=lax.Precision.HIGHEST)
-    both = sum_everywhere(jnp.concatenate([gram_part, cross_part]).reshape(64, 4, -1))
-    gram_sum, cross_sum = jnp.split(both.reshape(2 * total_members, total_members), 2)
-    factor = jnp.linalg.cholesky(
-        gram_sum + (total_members - 1.0) * jnp.eye(total_members, dtype=jnp.float32)
+    predicted, total = predict(
+        fields,
+        source.reshape(-1, layers),
+        wanted,
+        obs_values.reshape(1, layers),
+        obs_noise.reshape(-1, layers),
+        obs_var.reshape(1, layers),
     )
-    weights = jax.scipy.linalg.cho_solve((factor, True), cross_sum)
-    flat_field = ensemble.reshape(total_members, -1)
-    anomalies = flat_field - jnp.mean(flat_field, axis=0)
-    updated = flat_field + jnp.dot(weights.T, anomalies, precision=lax.Precision.HIGHEST)
-    return (updated.reshape(ensemble.shape), predicted)
+    updated = solve_and_update(total, fields)
+    return (updated.reshape(ensemble.shape), predicted.reshape(obs_noise.shape))
 
 
 def solution(mesh):

time: 146 us -> 123 us (0.84)
  other arithmetic: 25.8 us -> 0 us
  Pallas kernels: 112 us -> 120 us
  local copies, waits for them, and re-layouts: 4.83 us -> 1.15 us
  matrix products: 1.65 us -> 0 us
    another operation x5 -> x0, other arithmetic: 22.9 us -> none  [the longest x3 12.4 us: local(): jnp.linalg.cholesky(gram_sum + (total_members - 1.0) * jnp.eye(total_memb...]
    pallas_call x2, Pallas kernels: 112 us -> 120 us  [the longest x1 108 us: predict(): pl.pallas_call(conjugate_kernel, out_shape=[jax.ShapeDtypeStruct((rows, 1...]
    reduce_sum x2 -> x0, other arithmetic: 2.15 us -> none  [the longest x1 1.2 us: local(): anomalies = flat_field - jnp.mean(flat_field, axis=0)]
    unnamed x11 -> x3, local copies, waits for them, and re-layouts: 2.1 us -> 0.63 us
where the time goes in v4:
time: 123 us
  Pallas kernels  120 us (98%)
  between operations  1.29 us (1%)
    pallas_call x1, Pallas kernels, predict(): pl.pallas_call(conjugate_kernel, out_shape=[jax.ShapeDtypeStruct((rows, 1...  108 us
    pallas_call x1, Pallas kernels, solve_and_update(): pl.pallas_call(solve_kernel, out_shape=jax.ShapeDtypeStruct(ensemble.shap...  12.6 us

profile of v4, /device:TPU:1, one launch (start us, length us, event | category | flops | bytes accessed | tf_op | source)
XLA Modules:
  0.0 122.9 jit_solution(12490545337676512444)
XLA Ops:
  1.3 0.5 broadcast_in_dim.8.wanted
  1.8 107.8 %predict.1 = (f32[128,128]{1,0:T(8,128)}, f32[256,128]{1,0:T(8,128)}) custom-call(f32[1024,128]{1,0:T(8,128)} %bitcast.11, f32[8,128]{1,0:T(8,128)} %bitcast.16, s32[1,128]{1,0:T(1,128)} %broadcast_in_dim.8.wanted, f32[1,128]{1,0:T(1,128)} %bitcast.17, f32[128,128]{1,0:T(8,128)} %bitcast.15, f32[1,128]{1,0:T(1,128)} %bitcast.18), custom_call_target="tpu_custom_call" | custom-call | tf_op jit(solution)/shard_map/predict/pallas_call | solution.py:517
  109.6 0.0 copy-start
  109.6 12.6 %solve_and_update.1 = f32[1024,128]{1,0:T(8,128)} custom-call(f32[256,128]{1,0:T(8,128)} %get-tuple-element.4.total, f32[1024,128]{1,0:T(8,128)} %bitcast.12), custom_call_target="tpu_custom_call" | custom-call | tf_op jit(solution)/shard_map/solve_and_update/pallas_call | solution.py:630
  122.2 0.0 copy-done
  122.2 0.6 copy.11
Async XLA Ops:
  109.6 12.6 %copy-start = (f32[128,128]{1,0:T(8,128)S(1)}, f32[128,128]{1,0:T(8,128)}, u32[]{:S(2)}) copy-start(f32[128,128]{1,0:T(8,128)} %get-tuple-element.5) | copy-start | bytes 196612

commit v5 on v4

--- a/solution.py
+++ b/solution.py
@@ -252,14 +252,15 @@
     def send_sums(turn, norm, product):
         norm = norm + pltpu.roll(norm, 64, 1)
         product = product + pltpu.roll(product, 64, 1)
-        tiles[turn, member] = jnp.where(lane < 64, norm, product)
+        both = jnp.where(lane < 64, norm, product)
+        tiles[turn, member] = both[:4] + both[4:]
         for step in range(1, TEAM):
             tile_copy(turn, step).start()
 
     def sums_here(turn):
         wait_bytes(tiles.at[turn, pl.ds(0, TEAM - 1)], tile_recv.at[turn])
         both = jnp.sum(tiles[turn], axis=0)
-        both = both + pltpu.roll(both, 4, 0)
+        both = jnp.concatenate([both, both])
         norm = jnp.sum(jnp.where(lane < 64, both, 0.0), axis=1, keepdims=True)
         product = jnp.sum(jnp.where(lane < 64, 0.0, both), axis=1, keepdims=True)
         return jnp.broadcast_to(norm, plane), jnp.broadcast_to(product, plane)
@@ -356,12 +357,13 @@
         face_z[:, row] = upper
         lower_z[:, row] = jnp.where(lane_4 == 0, here, pltpu.roll(upper, 1, 2))
         face_y[1:4, row] = harmonic(here[:3], here[1:])
+        face_y[0, row] = here[0]
+        face_y[4, row] = here[3]
         return carry
 
     over_rows(inner_faces, 0)
     for y in range(4):
         face_x[y, 0] = harmonic(cond[y, 0], cond[y, 1])
-    edges_here(COND)
 
     def outer_faces(block, k, carry):
         row = 2 * block + k
@@ -369,14 +371,12 @@
         face_y[4, row] = harmonic(cond[3, row + 1], cond_edge[1, row])
         return carry
 
-    over_rows(outer_faces, 0)
-
-    def operate(lower_edge, upper_edge):
+    def operate():
         def body(block, k, carry):
             row = 2 * block + k
             here = searched[:, row + 1]
-            before = jnp.concatenate([lower_edge(block, k)[None], here[:3]])
-            after = jnp.concatenate([here[1:], upper_edge(block, k)[None]])
+            before = jnp.concatenate([here[:1], here[:3]])
+            after = jnp.concatenate([here[1:], here[3:]])
             result = face_x[:, row + 1] * (here - searched[:, row + 2])
             result = result + face_x[:, row] * (here - searched[:, row])
             result = result + face_y[1:5, row] * (here - after)
@@ -389,7 +389,31 @@
 
         over_rows(body, 0)
 
+    def operate_edges(lower_edge, upper_edge):
+        def body(block, k, carry):
+            row = 2 * block + k
+            image[0, row] = image[0, row] + face_y[0, row] * (searched[0, row + 1] - lower_edge(block, k))
+            image[3, row] = image[3, row] + face_y[4, row] * (searched[3, row + 1] - upper_edge(block, k))
+            return carry
+
+        over_rows(body, 0)
+
+    def over_planes(body, kind):
+        def outer(block, k, carry):
+            return body(slice(3, 4), 2 * block + k, body(slice(0, 1), 2 * block + k, carry))
+
+        def inner(block, k, carry):
+            return body(slice(1, 3), 2 * block + k, carry)
+
+        sums = over_rows(outer, (zeros, zeros))
+        if kind < ITERS - 1:
+            send_edges(kind)
+        return over_rows(inner, sums)
+
     zeros = jnp.zeros(plane, jnp.float32)
+    operate()
+    edges_here(COND)
+    over_rows(outer_faces, 0)
     edges_here(SOURCE)
 
     def source_side(upward):
@@ -399,30 +423,31 @@
 
         return rows
 
-    operate(source_side(0), source_side(1))
-
-    def first_sums(block, k, carry):
-        row = 2 * block + k
+    operate_edges(source_side(0), source_side(1))
+
+    def first_sums(ys, row, carry):
         norm, product = carry
-        image_here = image[:, row]
-        residual_here = searched[:, row + 1]
-        residual[:, row] = residual_here
-        searched[:, row + 1] = image_here
+        image_here = image[ys, row]
+        residual_here = searched[ys, row + 1]
+        residual[ys, row] = residual_here
+        searched[ys, row + 1] = image_here
         return norm + jnp.sum(residual_here * residual_here, axis=0), product + jnp.sum(
             residual_here * image_here, axis=0
         )
 
-    norm, product = over_rows(first_sums, (zeros, zeros))
+    norm, product = over_planes(first_sums, 0)
 
     norm_before = step_before = None
     for turn in range(ITERS):
         last = turn == ITERS - 1
         send_sums(turn, norm, product)
         if not last:
-            send_edges(turn)
             close_ends(searched, zeros)
+            operate()
             edges_here(turn)
-            operate(lambda block, k: edges[turn, 0, 2 * block + k], lambda block, k: edges[turn, 1, 2 * block + k])
+            operate_edges(
+                lambda block, k: edges[turn, 0, 2 * block + k], lambda block, k: edges[turn, 1, 2 * block + k]
+            )
         norm_now, product_now = sums_here(turn)
         if turn == 0:
             step_size = norm_now / product_now
@@ -431,25 +456,24 @@
             step_size = norm_now / (product_now - ratio * norm_now / step_before)
         norm_before, step_before = norm_now, step_size
 
-        def update(block, k, carry):
-            row = 2 * block + k
+        def update(ys, row, carry):
             norm, product = carry
-            residual_here, image_here = residual[:, row], searched[:, row + 1]
-            direction_here, along_here, beyond_here = residual_here, image_here, image[:, row]
+            residual_here, image_here = residual[ys, row], searched[ys, row + 1]
+            direction_here, along_here, beyond_here = residual_here, image_here, image[ys, row]
             answer_here = step_size * direction_here
             if turn > 0:
-                direction_here = direction_here + ratio * direction[:, row]
-                along_here = along_here + ratio * along[:, row]
-                beyond_here = beyond_here + ratio * beyond[:, row]
-                answer_here = answer[:, row] + step_size * direction_here
+                direction_here = direction_here + ratio * direction[ys, row]
+                along_here = along_here + ratio * along[ys, row]
+                beyond_here = beyond_here + ratio * beyond[ys, row]
+                answer_here = answer[ys, row] + step_size * direction_here
             residual_here = residual_here - step_size * along_here
             image_here = image_here - step_size * beyond_here
-            answer[:, row] = answer_here
-            direction[:, row] = direction_here
-            along[:, row] = along_here
-            beyond[:, row] = beyond_here
-            residual[:, row] = residual_here
-            searched[:, row + 1] = image_here
+            answer[ys, row] = answer_here
+            direction[ys, row] = direction_here
+            along[ys, row] = along_here
+            beyond[ys, row] = beyond_here
+            residual[ys, row] = residual_here
+            searched[ys, row + 1] = image_here
             return norm + jnp.sum(residual_here * residual_here, axis=0), product + jnp.sum(
                 residual_here * image_here, axis=0
             )
@@ -463,7 +487,7 @@
             over_rows(finish, 0)
         else:
             edges_sent(turn)
-            norm, product = over_rows(update, (zeros, zeros))
+            norm, product = over_planes(update, turn + 1)
 
     for block in range(HALF // 2):
         chosen = two_rows(held_wanted[block], held_wanted[HALF // 2 + block])
@@ -536,7 +560,7 @@
             vmem(2, HALF, 8, 128),
             vmem(2, HALF // 2, 4, 128),
             vmem(ITERS - 1, 2, HALF, 8, 128),
-            vmem(ITERS, TEAM, 8, 128),
+            vmem(ITERS, TEAM, 4, 128),
             pltpu.SemaphoreType.DMA((ITERS + 1, 2)),
             pltpu.SemaphoreType.DMA((ITERS + 1, 2)),
             pltpu.SemaphoreType.DMA((ITERS,)),

time: 123 us -> 118 us (0.959)
  Pallas kernels: 120 us -> 115 us
    pallas_call x1, Pallas kernels: 108 us -> 103 us  [predict(): pl.pallas_call(conjugate_kernel, out_shape=[jax.ShapeDtypeStruct((rows, 1...]
where the time goes in v5:
time: 118 us
  Pallas kernels  115 us (97%)
  between operations  1.29 us (1%)
    pallas_call x1, Pallas kernels, predict(): pl.pallas_call(conjugate_kernel, out_shape=[jax.ShapeDtypeStruct((rows, 1...  103 us
    pallas_call x1, Pallas kernels, solve_and_update(): pl.pallas_call(solve_kernel, out_shape=jax.ShapeDtypeStruct(ensemble.shap...  12.6 us

profile of v5, /device:TPU:1, one launch (start us, length us, event | category | flops | bytes accessed | tf_op | source)
XLA Modules:
  0.0 117.6 jit_solution(1076024942990002109)
XLA Ops:
  1.3 0.5 broadcast_in_dim.8.wanted
  1.8 102.6 %predict.1 = (f32[128,128]{1,0:T(8,128)}, f32[256,128]{1,0:T(8,128)}) custom-call(f32[1024,128]{1,0:T(8,128)} %bitcast.11, f32[8,128]{1,0:T(8,128)} %bitcast.16, s32[1,128]{1,0:T(1,128)} %broadcast_in_dim.8.wanted, f32[1,128]{1,0:T(1,128)} %bitcast.17, f32[128,128]{1,0:T(8,128)} %bitcast.15, f32[1,128]{1,0:T(1,128)} %bitcast.18), custom_call_target="tpu_custom_call" | custom-call | tf_op jit(solution)/shard_map/predict/pallas_call | solution.py:541
  104.3 0.0 copy-start
  104.4 12.6 %solve_and_update.1 = f32[1024,128]{1,0:T(8,128)} custom-call(f32[256,128]{1,0:T(8,128)} %get-tuple-element.4.total, f32[1024,128]{1,0:T(8,128)} %bitcast.12), custom_call_target="tpu_custom_call" | custom-call | tf_op jit(solution)/shard_map/solve_and_update/pallas_call | solution.py:654
  117.0 0.0 copy-done
  117.0 0.6 copy.11
Async XLA Ops:
  104.3 12.6 %copy-start = (f32[128,128]{1,0:T(8,128)S(1)}, f32[128,128]{1,0:T(8,128)}, u32[]{:S(2)}) copy-start(f32[128,128]{1,0:T(8,128)} %get-tuple-element.5) | copy-start | bytes 196612

commit v6 on v5

--- a/solution.py
+++ b/solution.py
@@ -151,6 +151,8 @@
     swap_send,
     swap_recv,
     own_sems,
+    relay_send,
+    relay_recv,
     part,
     *sum_refs,
 ):
@@ -237,17 +239,35 @@
             (wanted, held_wanted.at[space]),
         )
 
-    def swap(step):
-        other, device = space_peer(step)
-        for kind, (origin, target) in enumerate(piece_refs(other)):
-            pltpu.make_async_remote_copy(
-                src_ref=origin,
-                dst_ref=target,
-                send_sem=swap_send.at[kind],
-                recv_sem=swap_recv.at[kind],
-                device_id=device,
-                device_id_type=pl.DeviceIdType.MESH,
-            ).start()
+    def remote(origin, target, sends, receives, device):
+        return pltpu.make_async_remote_copy(
+            src_ref=origin,
+            dst_ref=target,
+            send_sem=sends,
+            recv_sem=receives,
+            device_id=device,
+            device_id_type=pl.DeviceIdType.MESH,
+        )
+
+    across = lax.rem(space + HALF // 2, SPACE)
+
+    def near_peer(step):
+        block, half = halves(space)
+        return {"space": half * (HALF // 2) + lax.rem(block + step, HALF // 2)}
+
+    def shared_refs():
+        block, half = halves(space)
+        for sender, side_of in ((space, half), (across, 1 - half)):
+            yield (
+                held_source.at[block, pl.ds(pl.multiple_of(side_of * 8, 8), 8)],
+                held_wanted.at[sender],
+            )
+
+    def relays():
+        return [
+            remote(origin, target, relay_send.at[kind], relay_recv.at[kind], {"space": across})
+            for kind, (origin, target) in enumerate(piece_refs(space)[1:])
+        ]
 
     def send_sums(turn, norm, product):
         norm = norm + pltpu.roll(norm, 64, 1)
@@ -288,8 +308,21 @@
     for copy in own:
         copy.start()
     pl.semaphore_wait(barrier, TEAM - 1 + SPACE - 1 + 3 * (WIDE - 1))
+    for copy in relays():
+        copy.start()
     for step in range(1, SPACE):
-        swap(step)
+        other, device = space_peer(step)
+        remote(*piece_refs(other)[0], swap_send.at[0], swap_recv.at[0], device).start()
+    mine, theirs = shared_refs()
+    for step in range(1, HALF // 2):
+        for kind, target in enumerate(mine):
+            origin = (source, wanted)[kind]
+            remote(origin, target, swap_send.at[1 + kind], swap_recv.at[1 + kind], near_peer(step)).start()
+    for copy in relays():
+        copy.wait_recv()
+    for step in range(1, HALF // 2):
+        for kind, target in enumerate(theirs):
+            remote(target, target, swap_send.at[1 + kind], swap_recv.at[1 + kind], near_peer(step)).start()
 
     @pl.when(member == 0)
     def _():
@@ -307,8 +340,8 @@
         copy.wait()
     others = SPACE - 1
     wait_bytes(ensemble.at[pl.ds(0, others * 32)], swap_recv.at[0])
-    wait_bytes(ensemble.at[pl.ds(0, others * 8)], swap_recv.at[1])
-    wait_bytes(held_wanted.at[pl.ds(0, others)], swap_recv.at[2])
+    wait_bytes(ensemble.at[pl.ds(0, (others - 1) * 8)], swap_recv.at[1])
+    wait_bytes(held_wanted.at[pl.ds(0, others - 1)], swap_recv.at[2])
 
     def two_rows(lower, upper):
         return jnp.where(low_half, jnp.broadcast_to(lower, plane), jnp.broadcast_to(upper, plane))
@@ -529,9 +562,11 @@
     for turn in range(ITERS):
         wait_bytes(tiles.at[turn, pl.ds(0, TEAM - 1)], tile_send.at[turn])
     wait_bytes(ensemble.at[pl.ds(0, others * 32)], swap_send.at[0])
-    wait_bytes(ensemble.at[pl.ds(0, others * 8)], swap_send.at[1])
-    wait_bytes(held_wanted.at[pl.ds(0, others)], swap_send.at[2])
+    wait_bytes(ensemble.at[pl.ds(0, (others - 1) * 8)], swap_send.at[1])
+    wait_bytes(held_wanted.at[pl.ds(0, others - 1)], swap_send.at[2])
     wait_bytes(returned.at[pl.ds(0, others)], swap_send.at[3])
+    for copy in relays():
+        copy.wait_send()
 
 
 def predict(ensemble, source, wanted, obs_values, obs_noise, obs_var):
@@ -568,6 +603,8 @@
             pltpu.SemaphoreType.DMA((4,)),
             pltpu.SemaphoreType.DMA((4,)),
             pltpu.SemaphoreType.DMA((3,)),
+            pltpu.SemaphoreType.DMA((2,)),
+            pltpu.SemaphoreType.DMA((2,)),
             vmem(64, 4, 128),
             vmem(WIDE - 1, WIDE, 4, 128),
             vmem(WIDE, 4, 128),

time: 118 us -> 114 us (0.966)
  Pallas kernels: 115 us -> 112 us
    pallas_call x1, Pallas kernels: 103 us -> 99.2 us  [predict(): pl.pallas_call(conjugate_kernel, out_shape=[jax.ShapeDtypeStruct((rows, 1...]
where the time goes in v6:
time: 114 us
  Pallas kernels  112 us (98%)
  between operations  1.29 us (1%)
  local copies, waits for them, and re-layouts  1.15 us (1%)
    pallas_call x1, Pallas kernels, predict(): pl.pallas_call(conjugate_kernel, out_shape=[jax.ShapeDtypeStruct((rows, 1...  99.2 us
    pallas_call x1, Pallas kernels, solve_and_update(): pl.pallas_call(solve_kernel, out_shape=jax.ShapeDtypeStruct(ensemble.shap...  12.6 us

profile of v6, /device:TPU:1, one launch (start us, length us, event | category | flops | bytes accessed | tf_op | source)
XLA Modules:
  0.0 114.3 jit_solution(3029298466103369039)
XLA Ops:
  1.3 0.5 broadcast_in_dim.8.wanted
  1.8 99.2 %predict.1 = (f32[128,128]{1,0:T(8,128)}, f32[256,128]{1,0:T(8,128)}) custom-call(f32[1024,128]{1,0:T(8,128)} %bitcast.11, f32[8,128]{1,0:T(8,128)} %bitcast.16, s32[1,128]{1,0:T(1,128)} %broadcast_in_dim.8.wanted, f32[1,128]{1,0:T(1,128)} %bitcast.17, f32[128,128]{1,0:T(8,128)} %bitcast.15, f32[1,128]{1,0:T(1,128)} %bitcast.18), custom_call_target="tpu_custom_call" | custom-call | tf_op jit(solution)/shard_map/predict/pallas_call | solution.py:576
  101.0 0.0 copy-start
  101.0 12.6 %solve_and_update.1 = f32[1024,128]{1,0:T(8,128)} custom-call(f32[256,128]{1,0:T(8,128)} %get-tuple-element.4.total, f32[1024,128]{1,0:T(8,128)} %bitcast.12), custom_call_target="tpu_custom_call" | custom-call | tf_op jit(solution)/shard_map/solve_and_update/pallas_call | solution.py:691
  113.6 0.0 copy-done
  113.6 0.6 copy.11
Async XLA Ops:
  101.0 12.6 %copy-start = (f32[128,128]{1,0:T(8,128)S(1)}, f32[128,128]{1,0:T(8,128)}, u32[]{:S(2)}) copy-start(f32[128,128]{1,0:T(8,128)} %get-tuple-element.5) | copy-start | bytes 196612

commit v7 on v6

--- a/solution.py
+++ b/solution.py
@@ -116,12 +116,13 @@
 def conjugate_kernel(
     ensemble,
     source,
-    wanted,
+    obs_row,
     obs_values,
     obs_noise,
     obs_var,
     predicted,
     total,
+    wanted,
     held_rows,
     held_source,
     held_wanted,
@@ -293,6 +294,7 @@
 
         return lax.fori_loop(0, HALF // 2, several, start)
 
+    wanted[...] = jnp.broadcast_to(obs_row[...], wanted.shape)
     barrier = pltpu.get_barrier_semaphore()
     for step in range(1, SPACE):
         pl.semaphore_signal(barrier, inc=1, device_id=space_peer(step)[1], device_id_type=pl.DeviceIdType.MESH)
@@ -569,7 +571,7 @@
         copy.wait_send()
 
 
-def predict(ensemble, source, wanted, obs_values, obs_noise, obs_var):
+def predict(ensemble, source, obs_row, obs_values, obs_noise, obs_var):
     held = (4, HALF, 8, 128)
     padded = (4, HALF + 2, 8, 128)
     vmem = lambda *shape: pltpu.VMEM(shape, jnp.float32)
@@ -579,6 +581,7 @@
         in_specs=[pl.BlockSpec(memory_space=pl.ANY), *[pl.BlockSpec(memory_space=pltpu.VMEM)] * 5],
         out_specs=[pl.BlockSpec(memory_space=pltpu.VMEM)] * 2,
         scratch_shapes=[
+            pltpu.VMEM((1, 128), jnp.int32),
             vmem(HALF // 2, 64, 128),
             vmem(HALF // 2, 16, 128),
             pltpu.VMEM((SPACE, 1, 128), jnp.int32),
@@ -618,13 +621,13 @@
         ],
         compiler_params=pltpu.CompilerParams(collective_id=2, has_side_effects=True),
         name="predict",
-    )(ensemble, source, wanted, obs_values, obs_noise, obs_var)
-
-
-PANEL = 8
-
-
-def solve_kernel(total, ensemble, updated, gram, cross, scaled, weights):
+    )(ensemble, source, obs_row, obs_values, obs_noise, obs_var)
+
+
+PANEL, GROUP = 8, 32
+
+
+def solve_kernel(total, ensemble, values, updated, predicted, gram, cross, scaled, weights):
     plane = (PANEL, 128)
     count = gram.shape[0]
     sublane = lax.broadcasted_iota(jnp.int32, plane, 0)
@@ -634,12 +637,21 @@
     def spread(row):
         return jnp.broadcast_to(row, plane)
 
+    predicted[...] = values[...]
     for low in range(0, count, PANEL):
         gram[low : low + PANEL] = total[low : low + PANEL] + jnp.where(lane == sublane + low, count - 1.0, 0.0)
     cross[...] = total[count:]
 
     for low in range(0, count, PANEL):
+        first = low - low % GROUP
         rows_g, rows_c = gram[low : low + PANEL], cross[low : low + PANEL]
+        for k in range(first, low):
+            if k % PANEL == 0:
+                held = rows_g
+            ahead = spread(held[:, k : k + 1])
+            rows_g = rows_g - ahead * spread(scaled[k : k + 1])
+            rows_c = rows_c - ahead * spread(weights[k : k + 1])
+        gram[low : low + PANEL] = rows_g
         columns = [spread(rows_g[:, low + j : low + j + 1]) for j in range(PANEL)]
         pivots = {(i, j): spread(columns[j][i : i + 1]) for j in range(PANEL) for i in range(j + 1)}
         inverse, factor = [], {}
@@ -666,15 +678,23 @@
         scaled[low : low + PANEL] = solved[0]
         weights[low : low + PANEL] = solved[1]
         after = low + PANEL
-        if after < count:
-            taken = rows_g.T
-            gram[after:] = gram[after:] - whole(taken, solved[0], (((1,), (0,)), ((), ())))[after:]
-            cross[after:] = cross[after:] - whole(taken, solved[1], (((1,), (0,)), ((), ())))[after:]
-
-    for low in range(count - 2 * PANEL, -1, -PANEL):
-        known = low + PANEL
-        left = jnp.where(lane >= known, scaled[low : low + PANEL], 0.0)
-        weights[low : low + PANEL] = weights[low : low + PANEL] - whole(left, weights[...], (((1,), (0,)), ((), ())))
+        if after % GROUP == 0 and after < count:
+            taken = gram[first:after].T
+            for target, factors in ((gram, scaled), (cross, weights)):
+                change = whole(taken, factors[first:after], (((1,), (0,)), ((), ())))
+                target[after:] = target[after:] - change[after:]
+
+    for first in range(count - GROUP, -1, -GROUP):
+        group = slice(first, first + GROUP)
+        if first + GROUP < count:
+            later = lax.broadcasted_iota(jnp.int32, (GROUP, count), 1) >= first + GROUP
+            left = jnp.where(later, scaled[group], 0.0)
+            weights[group] = weights[group] - whole(left, weights[...], (((1,), (0,)), ((), ())))
+        for low in range(first + GROUP - 2 * PANEL, first - 1, -PANEL):
+            rows_g, rows_c = scaled[low : low + PANEL], weights[low : low + PANEL]
+            for k in range(low + PANEL, first + GROUP):
+                rows_c = rows_c - spread(rows_g[:, k : k + 1]) * spread(weights[k : k + 1])
+            weights[low : low + PANEL] = rows_c
 
     turned = weights[...].T
     for row in range(PANEL):
@@ -686,31 +706,30 @@
             updated[pick, :] = fields[i] + change[PANEL * i : PANEL * (i + 1)]
 
 
-def solve_and_update(total, ensemble):
+def solve_and_update(total, ensemble, values):
     square = pltpu.VMEM((total.shape[1], total.shape[1]), jnp.float32)
     return pl.pallas_call(
         solve_kernel,
-        out_shape=jax.ShapeDtypeStruct(ensemble.shape, jnp.float32),
-        in_specs=[pl.BlockSpec(memory_space=pltpu.VMEM)] * 2,
-        out_specs=pl.BlockSpec(memory_space=pltpu.VMEM),
+        out_shape=[jax.ShapeDtypeStruct(array.shape, jnp.float32) for array in (ensemble, values)],
+        in_specs=[pl.BlockSpec(memory_space=pltpu.VMEM)] * 3,
+        out_specs=[pl.BlockSpec(memory_space=pltpu.VMEM)] * 2,
         scratch_shapes=[square] * 4,
         name="solve_and_update",
-    )(total, ensemble)
+    )(total, ensemble, values)
 
 
 def local(ensemble, source, obs_rows, obs_values, obs_noise, obs_var):
     layers = source.shape[-1]
     fields = ensemble.reshape(-1, layers)
-    wanted = jnp.broadcast_to(obs_rows.reshape(1, 1), (1, layers))
     predicted, total = predict(
         fields,
         source.reshape(-1, layers),
-        wanted,
+        obs_rows.reshape(1, 1),
         obs_values.reshape(1, layers),
         obs_noise.reshape(-1, layers),
         obs_var.reshape(1, layers),
     )
-    updated = solve_and_update(total, fields)
+    updated, predicted = solve_and_update(total, fields, predicted)
     return (updated.reshape(ensemble.shape), predicted.reshape(obs_noise.shape))
 
 

time: 114 us -> 109 us (0.956)
  Pallas kernels: 112 us -> 107 us
  local copies, waits for them, and re-layouts: 1.15 us -> 0 us
    pallas_call x1, Pallas kernels: 12.6 us -> 7.85 us  [solve_and_update(): pl.pallas_call(solve_kernel, out_shape=[jax.ShapeDtypeStruct(array.shape,...]
where the time goes in v7:
time: 109 us; the launch traced here: 108 us
  Pallas kernels  107 us (98%)
  between operations  1.28 us (1%)
    pallas_call x1, Pallas kernels, predict(): pl.pallas_call(conjugate_kernel, out_shape=[jax.ShapeDtypeStruct((rows, 1...  99.3 us
    pallas_call x1, Pallas kernels, solve_and_update(): pl.pallas_call(solve_kernel, out_shape=[jax.ShapeDtypeStruct(array.shape,...  7.85 us

profile of v7, /device:TPU:1, one launch (start us, length us, event | category | flops | bytes accessed | tf_op | source)
XLA Modules:
  0.0 108.4 jit_solution(11649886305631597156)
XLA Ops:
  1.3 99.3 %predict.1 = (f32[128,128]{1,0:T(8,128)}, f32[256,128]{1,0:T(8,128)}) custom-call(f32[1024,128]{1,0:T(8,128)} %bitcast.11, f32[8,128]{1,0:T(8,128)} %bitcast.14, s32[1,1]{1,0:T(1,128)} %bitcast.10.obs_row, f32[1,128]{1,0:T(1,128)} %bitcast.15, f32[128,128]{1,0:T(8,128)} %bitcast.13, f32[1,128]{1,0:T(1,128)} %bitcast.16), custom_call_target="tpu_custom_call" | custom-call | tf_op jit(solution)/shard_map/predict/pallas_call | solution.py:578
  100.6 7.8 %solve_and_update.1 = (f32[1024,128]{1,0:T(8,128)}, f32[128,128]{1,0:T(8,128)}) custom-call(f32[256,128]{1,0:T(8,128)} %get-tuple-element.6.total, f32[1024,128]{1,0:T(8,128)} %bitcast.12, f32[128,128]{1,0:T(8,128)} %get-tuple-element.7.values), custom_call_target="tpu_custom_call" | custom-call | tf_op jit(solution)/shard_map/solve_and_update/pallas_call | solution.py:711

commit v8 on v7

--- a/solution.py
+++ b/solution.py
@@ -287,12 +287,13 @@
         return jnp.broadcast_to(norm, plane), jnp.broadcast_to(product, plane)
 
     def over_rows(body, start):
-        def several(block, carry):
-            for k in range(2):
-                carry = body(block, k, carry)
+        def several(group, carry):
+            for i in range(4):
+                for k in range(2):
+                    carry = body(4 * group + i, k, carry)
             return carry
 
-        return lax.fori_loop(0, HALF // 2, several, start)
+        return lax.fori_loop(0, HALF // 8, several, start)
 
     wanted[...] = jnp.broadcast_to(obs_row[...], wanted.shape)
     barrier = pltpu.get_barrier_semaphore()

time: 109 us -> 108 us (level)
  no operation moved by 1% of the time
where the time goes in v8:
time: 108 us; the launch traced here: 107 us
  Pallas kernels  106 us (98%)
  between operations  1.28 us (1%)
    pallas_call x1, Pallas kernels, predict(): pl.pallas_call(conjugate_kernel, out_shape=[jax.ShapeDtypeStruct((rows, 1...  98.4 us
    pallas_call x1, Pallas kernels, solve_and_update(): pl.pallas_call(solve_kernel, out_shape=[jax.ShapeDtypeStruct(array.shape,...  7.85 us

profile of v8, /device:TPU:1, one launch (start us, length us, event | category | flops | bytes accessed | tf_op | source)
XLA Modules:
  0.0 107.5 jit_solution(16012271991838490876)
XLA Ops:
  1.3 98.4 %predict.1 = (f32[128,128]{1,0:T(8,128)}, f32[256,128]{1,0:T(8,128)}) custom-call(f32[1024,128]{1,0:T(8,128)} %bitcast.11, f32[8,128]{1,0:T(8,128)} %bitcast.14, s32[1,1]{1,0:T(1,128)} %bitcast.10.obs_row, f32[1,128]{1,0:T(1,128)} %bitcast.15, f32[128,128]{1,0:T(8,128)} %bitcast.13, f32[1,128]{1,0:T(1,128)} %bitcast.16), custom_call_target="tpu_custom_call" | custom-call | tf_op jit(solution)/shard_map/predict/pallas_call | solution.py:579
  99.6 7.8 %solve_and_update.1 = (f32[1024,128]{1,0:T(8,128)}, f32[128,128]{1,0:T(8,128)}) custom-call(f32[256,128]{1,0:T(8,128)} %get-tuple-element.6.total, f32[1024,128]{1,0:T(8,128)} %bitcast.12, f32[128,128]{1,0:T(8,128)} %get-tuple-element.7.values), custom_call_target="tpu_custom_call" | custom-call | tf_op jit(solution)/shard_map/solve_and_update/pallas_call | solution.py:712
